TPU v7x, 128 devices: a whole 4x4x4 slice. The times are simulated.
128 devices in a mesh: dp: 16 (over x, z_lo, core), ctx: 8 (over z_hi, y).
Axes of the slice: x: 4, y: 4, z: 4 (z_hi: 2, z_lo: 2; z = z_hi * 2 + z_lo), core: 2. Of those that a mesh axis runs over, the one named last changes fastest.
Arguments:
- document: bfloat16 [16, 2048, 1024], P('dp', 'ctx'), may hold values from -45 to 45, as said below
- summary: bfloat16 [16, 1024, 1024], P('dp', 'ctx'), may hold values from -45 to 45, as said below
- encoder_gain: float32 [1024], replicated, may hold values from 0.5 to 1.5
- query_weight: bfloat16 [1024, 1024], replicated, as said below
- key_weight: bfloat16 [1024, 1024], replicated, as said below
- value_weight: bfloat16 [1024, 1024], replicated, may hold values from -0.1875 to 0.1875
- output_weight: bfloat16 [1024, 1024], replicated, may hold values from -0.1875 to 0.1875
- memory_gain: float32 [1024], replicated, may hold values from 0.5 to 1.5
- summary_gain: float32 [1024], replicated, may hold values from 0.5 to 1.5
- cross_query: bfloat16 [1024, 1024], replicated, as said below
- cross_key: bfloat16 [1024, 1024], replicated, as said below
- cross_value: bfloat16 [1024, 1024], replicated, may hold values from -0.1875 to 0.1875
- cross_output: bfloat16 [1024, 1024], replicated, may hold values from -0.1875 to 0.1875
- encoder_cotangent: bfloat16 [16, 2048, 1024], P('dp', 'ctx'), as said below
- decoder_cotangent: bfloat16 [16, 1024, 1024], P('dp', 'ctx'), as said below
Outputs:
- encoded: bfloat16 [16, 2048, 1024], P('dp', 'ctx')
- decoded: bfloat16 [16, 1024, 1024], P('dp', 'ctx')
- output_grad: bfloat16 [1024, 1024], replicated
- cross_grad: bfloat16 [1024, 1024], replicated
Inputs may be any that keep to these rules, and one draw needn't show every extreme that they name: `document`: encoder states of order one. `summary`: decoder states of order one. `query_weight`: entries of order one over the square root of 1024. `key_weight`: entries of order one over the square root of 1024. `cross_query`: entries of order one over the square root of 1024. `cross_key`: entries of order one over the square root of 1024. `encoder_cotangent`: entries of order one over the square root of 32768. `decoder_cotangent`: entries of order one over the square root of 16384.
All inputs are finite; a program needn't handle non-finite values.
Results may differ from a plain program's by a relative error of at most 0.035.
The roundings to bfloat16 on the way count: a program that leaves them out, or rounds other values in their place, can miss the bound.
Values may be sent and summed in bfloat16 or wider, within the bound.
A program may use at most 192 MiB of HBM per device.

v0:
```python
import jax
import jax.numpy as jnp
from jax import lax
from jax.sharding import PartitionSpec as P

HEADS = 16
HEAD_DIM = 64


def norm_rows(rows, gain):
    values = rows.astype(jnp.float32)
    scale = lax.rsqrt(jnp.mean(values * values, axis=-1, keepdims=True) + 1e-06)
    return (values * scale * gain).astype(jnp.bfloat16)


def project(rows, weight):
    return jnp.dot(rows, weight, preferred_element_type=jnp.float32).astype(jnp.bfloat16)


def start_carry(count):
    best = jnp.full((HEADS, count), -jnp.inf, jnp.float32)
    total = jnp.zeros((HEADS, count), jnp.float32)
    accum = jnp.zeros((count, HEADS * HEAD_DIM), jnp.float32)
    return (best, total, accum)


def softmax_step(carry, query_heads, keys, values):
    best, total, accum = carry
    count = query_heads.shape[0]
    key_heads = keys.reshape(keys.shape[0], HEADS, HEAD_DIM)
    value_heads = values.reshape(values.shape[0], HEADS, HEAD_DIM)
    scores = jnp.einsum("qhd,khd->hqk", query_heads, key_heads, preferred_element_type=jnp.float32)
    new_best = jnp.max(scores, axis=-1)
    weights = jnp.exp(scores - new_best[:, :, None])
    decay = jnp.exp(best - new_best)
    total = total * decay + jnp.sum(weights, axis=-1)
    mixed = jnp.einsum(
        "hqk,khd->qhd",
        weights.astype(jnp.bfloat16),
        value_heads,
        preferred_element_type=jnp.float32,
    )
    accum = accum * jnp.repeat(jnp.transpose(decay), HEAD_DIM, axis=1) + mixed.reshape(
        count, HEADS * HEAD_DIM
    )
    return (new_best, total, accum)


def finish(carry):
    best, total, accum = carry
    return (accum / jnp.repeat(jnp.transpose(total), HEAD_DIM, axis=1)).astype(jnp.bfloat16)


def row_products(left, right):
    return lax.dot_general(
        left, right, (((0,), (0,)), ((), ())), preferred_element_type=jnp.float32
    )


def body(
    document,
    summary,
    encoder_gain,
    query_weight,
    key_weight,
    value_weight,
    output_weight,
    memory_gain,
    summary_gain,
    cross_query,
    cross_key,
    cross_value,
    cross_output,
    encoder_cotangent,
    decoder_cotangent,
):
    rows = document[0]
    states = summary[0]
    normed = norm_rows(rows, encoder_gain)
    query = project(normed, query_weight)
    keys = project(normed, key_weight)
    values = project(normed, value_weight)
    query_heads = query.reshape(rows.shape[0], HEADS, HEAD_DIM)
    piece = (
        lax.all_gather(keys, "ctx", axis=0, tiled=True),
        lax.all_gather(values, "ctx", axis=0, tiled=True),
    )
    heads = finish(softmax_step(start_carry(rows.shape[0]), query_heads, piece[0], piece[1]))
    own_local = row_products(heads, encoder_cotangent[0])
    encoded = (
        rows.astype(jnp.float32) + jnp.dot(heads, output_weight, preferred_element_type=jnp.float32)
    ).astype(jnp.bfloat16)
    memory = norm_rows(encoded, memory_gain)
    summary_query = project(norm_rows(states, summary_gain), cross_query)
    summary_heads = summary_query.reshape(states.shape[0], HEADS, HEAD_DIM)
    memory_keys = project(memory, cross_key)
    memory_values = project(memory, cross_value)
    piece = (
        lax.all_gather(memory_keys, "ctx", axis=0, tiled=True),
        lax.all_gather(memory_values, "ctx", axis=0, tiled=True),
    )
    folded = softmax_step(start_carry(states.shape[0]), summary_heads, piece[0], piece[1])
    cross_heads = finish(folded)
    decoded = (
        states.astype(jnp.float32)
        + jnp.dot(cross_heads, cross_output, preferred_element_type=jnp.float32)
    ).astype(jnp.bfloat16)
    cross_local = row_products(cross_heads, decoder_cotangent[0])
    own_sum, cross_sum = lax.psum((own_local, cross_local), ("dp", "ctx"))
    return (
        encoded[None],
        decoded[None],
        own_sum.astype(jnp.bfloat16),
        cross_sum.astype(jnp.bfloat16),
    )


def solution(mesh):
    in_specs = (
        P("dp", "ctx", None),
        P("dp", "ctx", None),
        P(),
        P(),
        P(),
        P(),
        P(),
        P(),
        P(),
        P(),
        P(),
        P(),
        P(),
        P("dp", "ctx", None),
        P("dp", "ctx", None),
    )
    out_specs = (P("dp", "ctx", None), P("dp", "ctx", None), P(), P())
    return jax.shard_map(body, mesh=mesh, in_specs=in_specs, out_specs=out_specs, check_vma=False)
```

profile of v0, /device:TPU:1, one launch (start us, length us, event | category | flops | bytes accessed | tf_op | source)
XLA Modules:
  0.0 465.5 jit_solution(679255280130076172)
XLA Ops:
  7.3 1.4 fusion.34
  8.6 3.3 convolution_convert_fusion.3
  12.1 3.1 convolution_convert_fusion.2
  15.3 3.1 convolution_convert_fusion.4
  18.4 1.2 copy.25
  19.7 66.9 %all-gather.5.cloned.1.call-done = bf16[2048,1024]{1,0:T(8,128)(2,1)} async-done(((bf16[256,1024]{1,0:T(8,128)(2,1)}), bf16[2048,1024]{1,0:T(8,128)(2,1)}) %all-gather.5.cloned.1.call-update) | async-done | bytes 4194320 | tf_op jit(solution)/shard_map/all_gather | solution.py:85
  86.6 6.5 %copy.26 = bf16[2048,1024]{0,1:T(8,128)(2,1)} copy(bf16[2048,1024]{1,0:T(8,128)(2,1)} %all-gather.5.cloned.1.call-done) | data formatting | bytes 8388608 | tf_op jit(solution)/shard_map/all_gather | solution.py:85
  93.1 15.6 %fusion.59 = (f32[16,256]{1,0:T(8,128)S(1)}, f32[16,256,2048]{2,1,0:T(8,128)}) fusion(bf16[256,16,64]{0,2,1:T(8,128)(2,1)S(1)} %bitcast.85, bf16[2048,16,64]{0,2,1:T(8,128)(2,1)} %bitcast.80), kind=kOutput, calls=%fused_computation.58 | convolution fusion | flops 1082126336 | bytes 38289408 | tf_op jit(solution)/shard_map/qhd,khd->hqk/dot_general | solution.py:32
  108.7 13.6 %fusion = f32[16,256]{1,0:T(8,128)S(1)} fusion(f32[16,256,2048]{2,1,0:T(8,128)} %get-tuple-element.7, f32[16,256]{1,0:T(8,128)S(1)} %get-tuple-element.6), kind=kLoop, calls=%fused_computation.1 | loop fusion | flops 16773120 | bytes 33587200 | tf_op jit(solution)/shard_map/reduce_sum | solution.py:36
  122.3 36.6 %all-gather.7.cloned.1.call-done = bf16[2048,1024]{1,0:T(8,128)(2,1)} async-done(((bf16[256,1024]{1,0:T(8,128)(2,1)}), bf16[2048,1024]{1,0:T(8,128)(2,1)}) %all-gather.7.cloned.1.call-update) | async-done | bytes 4194320 | tf_op jit(solution)/shard_map/all_gather | solution.py:86
  158.9 6.5 %copy.27 = bf16[2048,1024]{0,1:T(8,128)(2,1)} copy(bf16[2048,1024]{1,0:T(8,128)(2,1)} %all-gather.7.cloned.1.call-done) | data formatting | bytes 8388608 | tf_op jit(solution)/shard_map/all_gather | solution.py:86
  165.4 15.0 %fusion.27 = bf16[256,16,64]{0,2,1:T(8,128)(2,1)S(1)} fusion(bf16[2048,16,64]{0,2,1:T(8,128)(2,1)} %bitcast.81, f32[16,256,2048]{2,1,0:T(8,128)} %get-tuple-element.7, f32[16,256]{1,0:T(8,128)S(1)} %get-tuple-element.6, f32[256,16]{0,1:T(8,128)S(1)} %bitcast_add_fusion, f32[256,16]{0,1:T(8,128)S(1)} %multiply_bitcast_fusion), kind=kOutput, calls=%fused_computation.29 | convolution fusion | flops 1091305472 | bytes 38322176 | tf_op jit(solution)/shard_map/hqk,khd->qhd/dot_general | solution.py:37
  182.1 3.3 convolution_convert_fusion.1
  185.6 3.3 convolution_convert_fusion
  189.8 3.7 fusion.46
  193.5 61.4 %all-gather.9.cloned.1.call-done = bf16[2048,1024]{1,0:T(8,128)(2,1)} async-done(((bf16[256,1024]{1,0:T(8,128)(2,1)}), bf16[2048,1024]{1,0:T(8,128)(2,1)}) %all-gather.9.cloned.1.call-update) | async-done | bytes 4194320 | tf_op jit(solution)/shard_map/all_gather | solution.py:99
  254.9 6.4 %copy.29 = bf16[2048,1024]{0,1:T(8,128)(2,1)} copy(bf16[2048,1024]{1,0:T(8,128)(2,1)} %all-gather.9.cloned.1.call-done) | data formatting | bytes 8388608 | tf_op jit(solution)/shard_map/all_gather | solution.py:99
  261.3 10.3 %fusion.60 = (f32[16,128]{1,0:T(8,128)S(1)}, f32[16,128,2048]{2,1,0:T(8,128)}) fusion(bf16[128,16,64]{0,2,1:T(8,128)(2,1)S(1)} %bitcast.88, bf16[2048,16,64]{0,2,1:T(8,128)(2,1)} %bitcast.79), kind=kOutput, calls=%fused_computation.59 | convolution fusion | flops 541063168 | bytes 21241856 | tf_op jit(solution)/shard_map/qhd,khd->hqk/dot_general | solution.py:32
  271.7 8.2 %fusion.5 = f32[16,128]{1,0:T(8,128)S(1)} fusion(f32[16,128,2048]{2,1,0:T(8,128)} %get-tuple-element.11, f32[16,128]{1,0:T(8,128)S(1)} %get-tuple-element.10), kind=kLoop, calls=%fused_computation.6 | loop fusion | flops 8386560 | bytes 16793600 | tf_op jit(solution)/shard_map/reduce_sum | solution.py:36
  279.9 47.1 %all-gather.11.cloned.1.call-done = bf16[2048,1024]{1,0:T(8,128)(2,1)} async-done(((bf16[256,1024]{1,0:T(8,128)(2,1)}), bf16[2048,1024]{1,0:T(8,128)(2,1)}) %all-gather.11.cloned.1.call-update) | async-done | bytes 4194320 | tf_op jit(solution)/shard_map/all_gather | solution.py:100
  327.0 6.4 %copy.30 = bf16[2048,1024]{0,1:T(8,128)(2,1)} copy(bf16[2048,1024]{1,0:T(8,128)(2,1)} %all-gather.11.cloned.1.call-done) | data formatting | bytes 8388608 | tf_op jit(solution)/shard_map/all_gather | solution.py:100
  333.5 10.2 %fusion.40 = bf16[128,16,64]{0,2,1:T(8,128)(2,1)S(1)} fusion(bf16[2048,16,64]{0,2,1:T(8,128)(2,1)} %bitcast.82, f32[16,128,2048]{2,1,0:T(8,128)} %get-tuple-element.11, f32[16,128]{1,0:T(8,128)S(1)} %get-tuple-element.10, f32[128,16]{0,1:T(8,128)S(1)} %bitcast_add_fusion.1, f32[128,16]{0,1:T(8,128)S(1)} %multiply_bitcast_fusion.1), kind=kOutput, calls=%fused_computation.38 | convolution fusion | flops 545652736 | bytes 21258240 | tf_op jit(solution)/shard_map/hqk,khd->qhd/dot_general | solution.py:37
  343.7 2.6 fusion.49
  347.6 111.4 %all-reduce.2 = (bf16[1024,1024]{1,0:T(8,128)(2,1)}, bf16[1024,1024]{1,0:T(8,128)(2,1)}) all-reduce(f32[1024,1024]{1,0:T(8,128)} %fusion.46, f32[1024,1024]{1,0:T(8,128)} %fusion.49), channel_id=1, replica_groups=mesh['dp'=16,'ctx'=8] {'dp','ctx'}, use_global_device_ids=true, to_apply=%region_7.0 | all-reduce | flops 2097152 | bytes 12582912 | tf_op jit(solution)/shard_map/psum | solution.py:109
  (42 shorter events, 4.1 us)
Async XLA Ops:
  7.2 173.3 %copy-start = (bf16[1024,1024]{1,0:T(8,128)(2,1)S(1)}, bf16[1024,1024]{1,0:T(8,128)(2,1)}, u32[]{:S(2)}) copy-start(bf16[1024,1024]{1,0:T(8,128)(2,1)} %param.21) | copy-start | bytes 6291460
  7.2 4.9 %copy-start.5 = (bf16[1,256,1024]{2,1,0:T(8,128)(2,1)S(1)}, bf16[1,256,1024]{2,1,0:T(8,128)(2,1)}, u32[]{:S(2)}) copy-start(bf16[1,256,1024]{2,1,0:T(8,128)(2,1)} %param.15) | copy-start | bytes 1572868
  7.2 4.9 %copy-start.9 = (f32[1024]{0:T(1024)S(1)}, f32[1024]{0:T(1024)}, u32[]{:S(2)}) copy-start(f32[1024]{0:T(1024)} %param.17) | copy-start | bytes 12292
  7.2 79.4 %all-gather.5.cloned.1.call-start = ((), (), s32[]{:S(2)}) async-start(), calls=%async_computation | async-start | bytes 4718592 | tf_op jit(solution)/shard_map/all_gather | solution.py:85
  12.0 146.9 %all-gather.7.cloned.1.call-start = ((), (), s32[]{:S(2)}) async-start(), calls=%async_computation.1 | async-start | bytes 4718592 | tf_op jit(solution)/shard_map/all_gather | solution.py:86
  15.2 239.7 %all-gather.9.cloned.1.call-start = ((), (), s32[]{:S(2)}) async-start(), calls=%async_computation.2 | async-start | bytes 4718592 | tf_op jit(solution)/shard_map/all_gather | solution.py:99
  165.4 16.7 %copy-start.10 = (f32[1024]{0:T(1024)S(1)}, f32[1024]{0:T(1024)}, u32[]{:S(2)}) copy-start(f32[1024]{0:T(1024)} %param.22) | copy-start | bytes 12292
  181.3 0.8 copy-start.6
  182.1 6.9 %copy-start.2 = (bf16[1,128,1024]{2,1,0:T(8,128)(2,1)S(1)}, bf16[1,128,1024]{2,1,0:T(8,128)(2,1)}, u32[]{:S(2)}) copy-start(bf16[1,128,1024]{2,1,0:T(8,128)(2,1)} %param.16) | copy-start | bytes 786436
  182.1 7.1 %copy-start.3 = (bf16[1024,1024]{1,0:T(8,128)(2,1)S(1)}, bf16[1024,1024]{1,0:T(8,128)(2,1)}, u32[]{:S(2)}) copy-start(bf16[1024,1024]{1,0:T(8,128)(2,1)} %param.24) | copy-start | bytes 6291460
  182.1 7.1 %copy-start.8 = (f32[1024]{0:T(1024)S(1)}, f32[1024]{0:T(1024)}, u32[]{:S(2)}) copy-start(f32[1024]{0:T(1024)} %param.23) | copy-start | bytes 12292
  185.4 141.6 %all-gather.11.cloned.1.call-start = ((), (), s32[]{:S(2)}) async-start(), calls=%async_computation.3 | async-start | bytes 4718592 | tf_op jit(solution)/shard_map/all_gather | solution.py:100
  333.5 10.3 %copy-start.7 = (bf16[1,128,1024]{2,1,0:T(8,128)(2,1)S(1)}, bf16[1,128,1024]{2,1,0:T(8,128)(2,1)}, u32[]{:S(2)}) copy-start(bf16[1,128,1024]{2,1,0:T(8,128)(2,1)} %param.29) | copy-start | bytes 786436
  343.7 2.7 copy-start.4
  346.4 112.6 %copy-start.1 = (bf16[1024,1024]{1,0:T(8,128)(2,1)S(1)}, bf16[1024,1024]{1,0:T(8,128)(2,1)}, u32[]{:S(2)}) copy-start(bf16[1024,1024]{1,0:T(8,128)(2,1)} %param.21) | copy-start | bytes 6291460
Sparse Core Ops, SparseCore 0:
  12.1 74.4 all-gather.4
  89.5 69.3 all-gather.6
  185.5 69.3 all-gather.8
  257.7 69.3 all-gather.10
where the time goes:
time: 468 us; the launch traced here: 466 us
  waiting for transfers between devices  212 us (45%)
  blocking collectives  111 us (24%)
  matrix products  76.3 us (16%)
  local copies, waits for them, and re-layouts  28.1 us (6%)
  other arithmetic  23.4 us (5%)
  between operations  13.9 us (3%)
    psum x1, blocking collectives, body(): own_sum, cross_sum = lax.psum((own_local, cross_local), ('dp', 'ctx'))  111 us
    all_gather x1, waiting for transfers between devices, body(): lax.all_gather(keys, 'ctx', axis=0, tiled=True)  66.9 us
    all_gather x1, waiting for transfers between devices, body(): lax.all_gather(memory_keys, 'ctx', axis=0, tiled=True)  61.4 us
    all_gather x1, waiting for transfers between devices, body(): lax.all_gather(memory_values, 'ctx', axis=0, tiled=True)  47.1 us
    all_gather x1, waiting for transfers between devices, body(): lax.all_gather(values, 'ctx', axis=0, tiled=True)  36.6 us
    dot_general x2, matrix products, softmax_step(): jnp.einsum('qhd,khd->hqk', query_heads, key_heads, preferred_element_type...  25.9 us
    dot_general x2, matrix products, softmax_step(): jnp.einsum('hqk,khd->qhd', weights.astype(jnp.bfloat16), value_heads, pre...  25.3 us
    reduce_sum x2, other arithmetic, softmax_step(): total = total * decay + jnp.sum(weights, axis=-1)  21.8 us
  transfers between devices with their start and end apart: 4, of which 4 were waited for; matrix products, arithmetic and copies ran while one was open for 16% of the time, Pallas kernels for 0%

commit v1 on v0

v1 whole, which is shorter than its diff:
```python
import functools

import jax
import jax.numpy as jnp
from jax import lax
from jax.experimental import pallas as pl
from jax.experimental.pallas import tpu as pltpu
from jax.sharding import PartitionSpec as P

HEADS = 16
HEAD_DIM = 64
LANES = 128
MESH = pl.DeviceIdType.MESH
QKV, SQ, HEAD, KV, CROSS = range(5)


def norm_rows(rows, gain):
    values = rows.astype(jnp.float32)
    scale = lax.rsqrt(jnp.mean(values * values, axis=-1, keepdims=True) + 1e-06)
    return (values * scale * gain).astype(jnp.bfloat16)


def matmul(left, right):
    return jnp.dot(left, right, preferred_element_type=jnp.float32)


def layer_kernel(
    n,
    document,
    summary,
    encoder_gain,
    memory_gain,
    summary_gain,
    query_weight,
    key_weight,
    value_weight,
    output_weight,
    cross_query,
    cross_key,
    cross_value,
    cross_output,
    encoded_out,
    decoded_out,
    heads_out,
    cross_out,
    doc,
    states,
    weights,
    normed,
    qkv_send,
    qkv_recv,
    sq_send,
    sq_recv,
    head_send,
    head_recv,
    kv_send,
    kv_recv,
    cross_send,
    cross_recv,
    value_low,
    value_high,
    encoded,
    decoded,
    load_sem,
    store_sem,
    send_sem,
    recv_sem,
):
    dp = lax.axis_index("dp")
    me = lax.axis_index("ctx")
    rows = doc.shape[0]
    count = states.shape[0]
    width = doc.shape[1]
    blocks = width // (2 * LANES)

    loads = [
        pltpu.make_async_copy(src, dst, load_sem.at[i])
        for i, (src, dst) in enumerate(
            [
                (document, doc),
                (query_weight, weights.at[0]),
                (key_weight, weights.at[1]),
                (value_weight, weights.at[2]),
                (summary, states),
                (cross_query, weights.at[4]),
                (output_weight, weights.at[3]),
                (cross_key, weights.at[5]),
                (cross_value, weights.at[6]),
                (cross_output, weights.at[7]),
            ]
        )
    ]
    for load in loads:
        load.start()

    barrier = pltpu.get_barrier_semaphore()

    @pl.loop(1, n)
    def _(i):
        peer = lax.rem(me + i, n)
        pl.semaphore_signal(barrier, inc=1, device_id=(dp, peer), device_id_type=MESH)

    def remote(phase, peer, source, src, dst):
        return pltpu.make_async_remote_copy(
            src_ref=src,
            dst_ref=dst,
            send_sem=send_sem.at[phase, peer],
            recv_sem=recv_sem.at[phase, source],
            device_id=(dp, peer),
            device_id_type=MESH,
        )

    def local(phase, src, dst):
        return pltpu.make_async_copy(src, dst, recv_sem.at[phase, me])

    def start(phase, peer, src, dst):
        @pl.when(peer != me)
        def _():
            remote(phase, peer, me, src, dst).start()

        @pl.when(peer == me)
        def _():
            local(phase, src, dst).start()

    def wait_all(phase, src_of, dst_of):
        @pl.loop(0, n)
        def _(source):
            @pl.when(source != me)
            def _():
                remote(phase, source, source, src_of(source), dst_of(source)).wait_recv()

            @pl.when(source == me)
            def _():
                local(phase, src_of(source), dst_of(source)).wait()

    def wait_sent(phase, src_of, dst_of):
        @pl.loop(0, n)
        def _(peer):
            @pl.when(peer != me)
            def _():
                remote(phase, peer, me, src_of(peer), dst_of(peer)).wait_send()

    def column(index):
        return pl.ds(pl.multiple_of(index * LANES, LANES), LANES)

    def wide(index):
        return pl.ds(pl.multiple_of(index * 2 * LANES, 2 * LANES), 2 * LANES)

    loads[0].wait()
    normed[...] = norm_rows(doc[...], encoder_gain[...])
    for i in (1, 2, 3):
        loads[i].wait()
    pl.semaphore_wait(barrier, n - 1)

    @pl.loop(0, blocks)
    def _(i):
        block = lax.rem(lax.div(me, 2) + (blocks - 1) - i, blocks)
        for t in range(3):
            part = matmul(normed[...], weights[t, :, wide(block)]).astype(jnp.bfloat16)
            qkv_send[2 * block, t] = part[:, :LANES]
            qkv_send[2 * block + 1, t] = part[:, LANES:]
        for half in range(2):
            peer = 2 * block + half
            start(QKV, peer, qkv_send.at[peer], qkv_recv.at[:, me])

    loads[4].wait()
    loads[5].wait()
    normed[0:count, :] = norm_rows(states[...], summary_gain[...])

    @pl.loop(0, blocks)
    def _(i):
        block = lax.rem(lax.div(me, 2) + (blocks - 1) - i, blocks)
        part = matmul(normed[0:count, :], weights[4, :, wide(block)]).astype(jnp.bfloat16)
        sq_send[2 * block] = part[:, :LANES]
        sq_send[2 * block + 1] = part[:, LANES:]
        for half in range(2):
            peer = 2 * block + half
            start(SQ, peer, sq_send.at[peer], sq_recv.at[me])

    lane = lax.broadcasted_iota(jnp.int32, (1, LANES), 1)
    low = lane < HEAD_DIM
    zero = jnp.zeros((), jnp.bfloat16)
    one = jnp.ones((), jnp.bfloat16)

    def set_values(ref):
        values = ref[...].reshape(n * rows, LANES)
        value_low[...] = jnp.where(low, values, one)
        value_high[...] = jnp.where(low, one, values)

    def attend(query, keys):
        def head(part, values):
            scores = lax.dot_general(
                part, keys, (((1,), (1,)), ((), ())), preferred_element_type=jnp.float32
            )
            top = jnp.max(scores, axis=-1, keepdims=True)
            weight = jnp.exp(scores - top).astype(jnp.bfloat16)
            return matmul(weight, values[...])

        left = head(jnp.where(low, query, zero), value_low)
        right = head(jnp.where(low, zero, query), value_high)
        mixed = jnp.where(low, left, right)
        total = jnp.where(
            low, pltpu.roll(left, HEAD_DIM, 1), pltpu.roll(right, HEAD_DIM, 1)
        )
        return (mixed / total).astype(jnp.bfloat16)

    wait_all(QKV, lambda s: qkv_send.at[s], lambda s: qkv_recv.at[:, s])
    set_values(qkv_recv.at[2])

    @pl.loop(0, n)
    def _(i):
        peer = lax.rem(me + 1 + i, n)
        keys = qkv_recv[1].reshape(n * rows, LANES)
        head_send[peer] = attend(qkv_recv[0, peer], keys)
        start(HEAD, peer, head_send.at[peer], head_recv.at[:, column(me)])

    loads[6].wait()
    wait_all(HEAD, lambda s: head_send.at[s], lambda s: head_recv.at[:, column(s)])

    @pl.loop(0, blocks)
    def _(i):
        mixed = matmul(head_recv[...], weights[3, :, wide(i)])
        encoded[:, wide(i)] = (doc[:, wide(i)].astype(jnp.float32) + mixed).astype(jnp.bfloat16)

    stores = [
        pltpu.make_async_copy(src, dst, store_sem.at[i])
        for i, (src, dst) in enumerate(
            [
                (encoded, encoded_out),
                (head_recv, heads_out),
                (decoded, decoded_out),
                (cross_recv, cross_out),
            ]
        )
    ]
    stores[0].start()
    stores[1].start()

    normed[...] = norm_rows(encoded[...], memory_gain[...])
    loads[7].wait()
    loads[8].wait()

    @pl.loop(0, blocks)
    def _(i):
        block = lax.rem(lax.div(me, 2) + (blocks - 1) - i, blocks)
        for t in range(2):
            part = matmul(normed[...], weights[5 + t, :, wide(block)]).astype(jnp.bfloat16)
            kv_send[2 * block, t] = part[:, :LANES]
            kv_send[2 * block + 1, t] = part[:, LANES:]
        for half in range(2):
            peer = 2 * block + half
            start(KV, peer, kv_send.at[peer], kv_recv.at[:, me])

    wait_all(SQ, lambda s: sq_send.at[s], lambda s: sq_recv.at[s])
    wait_all(KV, lambda s: kv_send.at[s], lambda s: kv_recv.at[:, s])
    set_values(kv_recv.at[1])

    @pl.loop(0, n // 2)
    def _(i):
        pair = lax.rem(lax.div(me, 2) + 1 + i, n // 2)
        keys = kv_recv[0].reshape(n * rows, LANES)
        query = sq_recv[pl.ds(2 * pair, 2)].reshape(2 * count, LANES)
        mixed = attend(query, keys)
        cross_send[2 * pair] = mixed[:count]
        cross_send[2 * pair + 1] = mixed[count:]
        for half in range(2):
            peer = 2 * pair + half
            start(CROSS, peer, cross_send.at[peer], cross_recv.at[:, column(me)])

    loads[9].wait()
    wait_all(CROSS, lambda s: cross_send.at[s], lambda s: cross_recv.at[:, column(s)])

    @pl.loop(0, blocks)
    def _(i):
        mixed = matmul(cross_recv[...], weights[7, :, wide(i)])
        decoded[:, wide(i)] = (states[:, wide(i)].astype(jnp.float32) + mixed).astype(jnp.bfloat16)

    stores[2].start()
    stores[3].start()
    wait_sent(QKV, lambda p: qkv_send.at[p], lambda p: qkv_recv.at[:, me])
    wait_sent(SQ, lambda p: sq_send.at[p], lambda p: sq_recv.at[me])
    wait_sent(HEAD, lambda p: head_send.at[p], lambda p: head_recv.at[:, column(me)])
    wait_sent(KV, lambda p: kv_send.at[p], lambda p: kv_recv.at[:, me])
    wait_sent(CROSS, lambda p: cross_send.at[p], lambda p: cross_recv.at[:, column(me)])
    for store in stores:
        store.wait()


def row_products(left, right):
    return lax.dot_general(
        left, right, (((0,), (0,)), ((), ())), preferred_element_type=jnp.float32
    )


def solution(mesh):
    n = mesh.shape["ctx"]

    def body(
        document,
        summary,
        encoder_gain,
        query_weight,
        key_weight,
        value_weight,
        output_weight,
        memory_gain,
        summary_gain,
        cross_query,
        cross_key,
        cross_value,
        cross_output,
        encoder_cotangent,
        decoder_cotangent,
    ):
        rows, width = document.shape[1:]
        count = summary.shape[1]
        half = jnp.bfloat16
        hbm = pl.BlockSpec(memory_space=pl.ANY)
        vmem = pl.BlockSpec(memory_space=pltpu.VMEM)
        encoded, decoded, heads, cross_heads = pl.pallas_call(
            functools.partial(layer_kernel, n),
            out_shape=[
                jax.ShapeDtypeStruct((rows, width), half),
                jax.ShapeDtypeStruct((count, width), half),
                jax.ShapeDtypeStruct((rows, width), half),
                jax.ShapeDtypeStruct((count, width), half),
            ],
            in_specs=[hbm] * 2 + [vmem] * 3 + [hbm] * 8,
            out_specs=[hbm] * 4,
            scratch_shapes=[
                pltpu.VMEM((rows, width), half),
                pltpu.VMEM((count, width), half),
                pltpu.VMEM((8, width, width), half),
                pltpu.VMEM((rows, width), half),
                pltpu.VMEM((n, 3, rows, LANES), half),
                pltpu.VMEM((3, n, rows, LANES), half),
                pltpu.VMEM((n, count, LANES), half),
                pltpu.VMEM((n, count, LANES), half),
                pltpu.VMEM((n, rows, LANES), half),
                pltpu.VMEM((rows, width), half),
                pltpu.VMEM((n, 2, rows, LANES), half),
                pltpu.VMEM((2, n, rows, LANES), half),
                pltpu.VMEM((n, count, LANES), half),
                pltpu.VMEM((count, width), half),
                pltpu.VMEM((n * rows, LANES), half),
                pltpu.VMEM((n * rows, LANES), half),
                pltpu.VMEM((rows, width), half),
                pltpu.VMEM((count, width), half),
                pltpu.SemaphoreType.DMA((10,)),
                pltpu.SemaphoreType.DMA((4,)),
                pltpu.SemaphoreType.DMA((5, n)),
                pltpu.SemaphoreType.DMA((5, n)),
            ],
            compiler_params=pltpu.CompilerParams(
                collective_id=0, has_side_effects=True, vmem_limit_bytes=56 * 2**20
            ),
        )(
            document[0],
            summary[0],
            encoder_gain[None],
            memory_gain[None],
            summary_gain[None],
            query_weight,
            key_weight,
            value_weight,
            output_weight,
            cross_query,
            cross_key,
            cross_value,
            cross_output,
        )
        own_local = row_products(heads, encoder_cotangent[0])
        cross_local = row_products(cross_heads, decoder_cotangent[0])
        own_sum, cross_sum = lax.psum((own_local, cross_local), ("dp", "ctx"))
        return (
            encoded[None],
            decoded[None],
            own_sum.astype(jnp.bfloat16),
            cross_sum.astype(jnp.bfloat16),
        )

    rows_spec = P("dp", "ctx", None)
    return jax.shard_map(
        body,
        mesh=mesh,
        in_specs=(rows_spec, rows_spec) + (P(),) * 11 + (rows_spec, rows_spec),
        out_specs=(rows_spec, rows_spec, P(), P()),
        check_vma=False,
    )
```

time: 468 us -> 195 us (0.42)
  waiting for transfers between devices: 212 us -> 0 us
  Pallas kernels: 0 us -> 71.1 us
  matrix products: 76.3 us -> 6.48 us
  local copies, waits for them, and re-layouts: 28.1 us -> 1.52 us
  other arithmetic: 23.4 us -> 0 us
  between operations: 13.9 us -> 0.68 us
    all_gather x4 -> x0, waiting for transfers between devices: 212 us -> none  [the longest x1 66.9 us: body(): lax.all_gather(keys, 'ctx', axis=0, tiled=True)]
    pallas_call x0 -> x1, Pallas kernels: none -> 71.1 us  [body(): pl.pallas_call(functools.partial(layer_kernel, n), out_shape=[jax.ShapeDt...]
    dot_general x12 -> x0, matrix products: 70 us -> none  [the longest x2 25.9 us: softmax_step(): jnp.einsum('qhd,khd->hqk', query_heads, key_heads, preferred_element_type...]
    all_gather x4 -> x0, local copies, waits for them, and re-layouts: 25.9 us -> none  [the longest x1 6.5 us: body(): lax.all_gather(keys, 'ctx', axis=0, tiled=True)]
    reduce_sum x4 -> x0, other arithmetic: 23.3 us -> none  [the longest x2 21.8 us: softmax_step(): total = total * decay + jnp.sum(weights, axis=-1)]
  transfers between devices with their start and end apart: 4 -> 0, of which waited for: 4 -> 0; matrix products, arithmetic and copies ran while one was open for 16% -> 0% of each run, Pallas kernels for 0% -> 0%
where the time goes in v1:
time: 195 us; the launch traced here: 194 us
  blocking collectives  114 us (58%)
  Pallas kernels  71.1 us (36%)
  matrix products  6.48 us (3%)
    psum x1, blocking collectives, body(): own_sum, cross_sum = lax.psum((own_local, cross_local), ('dp', 'ctx'))  114 us
    pallas_call x1, Pallas kernels, body(): pl.pallas_call(functools.partial(layer_kernel, n), out_shape=[jax.ShapeDt...  71.1 us
    dot_general x2, matrix products, row_products(): lax.dot_general(left, right, (((0,), (0,)), ((), ())), preferred_element_...  6.48 us

profile of v1, /device:TPU:1, one launch (start us, length us, event | category | flops | bytes accessed | tf_op | source)
XLA Modules:
  0.0 193.6 jit_solution(7116723173921970585)
XLA Ops:
  0.6 0.0 copy-start
  0.7 71.1 %shard_map.174 = (bf16[256,1024]{1,0:T(8,128)(2,1)}, bf16[128,1024]{1,0:T(8,128)(2,1)}, bf16[256,1024]{1,0:T(8,128)(2,1)}, bf16[128,1024]{1,0:T(8,128)(2,1)}) custom-call(bf16[256,1024]{1,0:T(8,128)(2,1)} %bitcast.15, bf16[128,1024]{1,0:T(8,128)(2,1)} %bitcast.17, f32[1,1024]{1,0:T(1,128)} %bitcast.19, f32[1,1024]{1,0:T(1,128)} %bitcast.20, ...), custom_call_target="tpu_custom_call" | custom-call | tf_op jit(solution)/shard_map/pallas_call | solution.py:320
  71.7 0.0 copy-done
  71.7 0.0 copy-start.2
  71.7 0.0 copy-start.3
  71.7 3.8 %fusion = f32[1024,1024]{1,0:T(8,128)} fusion(bf16[256,1024]{1,0:T(8,128)(2,1)} %get-tuple-element.10, bf16[1,256,1024]{2,1,0:T(8,128)(2,1)S(1)} %copy-done), kind=kOutput, calls=%fused_computation | convolution fusion | flops 536870912 | bytes 5242880 | tf_op jit(solution)/shard_map/dot_general | solution.py:290
  75.5 0.0 copy-done.2
  75.5 0.0 copy-done.3
  75.5 2.7 %fusion.2 = f32[1024,1024]{1,0:T(8,128)} fusion(bf16[128,1024]{1,0:T(8,128)(2,1)S(1)} %copy-done.3, bf16[1,128,1024]{2,1,0:T(8,128)(2,1)S(1)} %copy-done.2), kind=kOutput, calls=%fused_computation.2 | convolution fusion | flops 268435456 | bytes 4718592 | tf_op jit(solution)/shard_map/dot_general | solution.py:290
  78.2 0.0 copy-start.1
  78.2 0.0 copy-start.4
  78.2 113.9 %all-reduce.2 = (bf16[1024,1024]{1,0:T(8,128)(2,1)}, bf16[1024,1024]{1,0:T(8,128)(2,1)}) all-reduce(f32[1024,1024]{1,0:T(8,128)} %fusion, f32[1024,1024]{1,0:T(8,128)} %fusion.2), channel_id=1, replica_groups=mesh['dp'=16,'ctx'=8] {'dp','ctx'}, use_global_device_ids=true, to_apply=%region_0.0 | all-reduce | flops 2097152 | bytes 12582912 | tf_op jit(solution)/shard_map/psum | solution.py:374
  192.1 0.0 copy-done.1
  192.1 0.8 copy.25
  192.9 0.0 copy-done.4
  192.9 0.7 copy.26
Async XLA Ops:
  0.6 71.1 %copy-start = (bf16[1,256,1024]{2,1,0:T(8,128)(2,1)S(1)}, bf16[1,256,1024]{2,1,0:T(8,128)(2,1)}, u32[]{:S(2)}) copy-start(bf16[1,256,1024]{2,1,0:T(8,128)(2,1)} %param.28) | copy-start | bytes 1572868
  71.7 3.8 %copy-start.2 = (bf16[1,128,1024]{2,1,0:T(8,128)(2,1)S(1)}, bf16[1,128,1024]{2,1,0:T(8,128)(2,1)}, u32[]{:S(2)}) copy-start(bf16[1,128,1024]{2,1,0:T(8,128)(2,1)} %param.29) | copy-start | bytes 786436
  71.7 3.8 %copy-start.3 = (bf16[128,1024]{1,0:T(8,128)(2,1)S(1)}, bf16[128,1024]{1,0:T(8,128)(2,1)}, u32[]{:S(2)}) copy-start(bf16[128,1024]{1,0:T(8,128)(2,1)} %get-tuple-element.11) | copy-start | bytes 786436
  78.2 113.9 %copy-start.1 = (bf16[256,1024]{1,0:T(8,128)(2,1)S(1)}, bf16[256,1024]{1,0:T(8,128)(2,1)}, u32[]{:S(2)}) copy-start(bf16[256,1024]{1,0:T(8,128)(2,1)} %get-tuple-element.8) | copy-start | bytes 1572868
  78.2 114.7 %copy-start.4 = (bf16[128,1024]{1,0:T(8,128)(2,1)S(1)}, bf16[128,1024]{1,0:T(8,128)(2,1)}, u32[]{:S(2)}) copy-start(bf16[128,1024]{1,0:T(8,128)(2,1)} %get-tuple-element.9) | copy-start | bytes 786436

commit v2 on v1

--- a/solution.py
+++ b/solution.py
@@ -22,6 +22,232 @@
 
 def matmul(left, right):
     return jnp.dot(left, right, preferred_element_type=jnp.float32)
+
+
+OWN_PARTS = ((0, 1024, "xyz"),)
+CROSS_PARTS = ((0, 512, "xyz"), (512, 256, "yzx"), (768, 256, "zxy"))
+REFS = 11
+
+
+class Neighbours:
+    def __init__(self, dp, ctx):
+        self.core = lax.rem(dp, 2)
+        self.x = lax.div(dp, 4)
+        self.y = lax.rem(ctx, 4)
+        self.z = lax.div(ctx, 4) * 2 + lax.rem(lax.div(dp, 2), 2)
+        self.sibling = self.device(self.x, self.y, self.z, 1 - self.core)
+
+    def device(self, x, y, z, core):
+        return (x * 4 + lax.rem(z, 2) * 2 + core, lax.div(z, 2) * 4 + y)
+
+    def place(self, axis):
+        return {"x": self.x, "y": self.y, "z": self.z}[axis]
+
+    def at(self, axis, step):
+        place = {"x": self.x, "y": self.y, "z": self.z}
+        place[axis] = lax.rem(place[axis] + step, 4)
+        return self.device(place["x"], place["y"], place["z"], self.core)
+
+
+def aligned(start, size):
+    return pl.ds(pl.multiple_of(start, size), size)
+
+
+class Reduction:
+    def __init__(
+        self, near, parts, partial, pair, first, first_in, second, second_in, third, third_in, full, send, recv
+    ):
+        self.near = near
+        self.parts = parts
+        self.partial, self.pair, self.full = partial, pair, full
+        self.held = [first, second, third]
+        self.incoming = [first_in, second_in, third_in]
+        self.send, self.recv = send, recv
+        self.half = pair.shape[0]
+        self.base = near.core * self.half
+        self.started = []
+
+    def copy(self, src, dst, slot, device):
+        return pltpu.make_async_remote_copy(
+            src_ref=src,
+            dst_ref=dst,
+            send_sem=self.send.at[slot],
+            recv_sem=self.recv.at[slot],
+            device_id=device,
+            device_id_type=MESH,
+        )
+
+    def product(self, left, right):
+        step = 256
+
+        @pl.loop(0, left.shape[1] // step)
+        def _(i):
+            block = lax.rem(i + (1 - self.near.core) * (self.half // step), left.shape[1] // step)
+            rows = aligned(block * step, step)
+            mixed = lax.dot_general(
+                left[:, rows], right[...], (((0,), (0,)), ((), ())), preferred_element_type=jnp.float32
+            )
+            self.partial[rows, :] = mixed.astype(jnp.bfloat16)
+
+        other = (1 - self.near.core) * self.half
+        self.pair_copy = self.copy(
+            self.partial.at[aligned(other, self.half)], self.pair, 0, self.near.sibling
+        )
+        self.pair_copy.start()
+        self.started.append(self.pair_copy)
+
+    def pair_sum(self):
+        self.pair_copy.wait_recv()
+        step = 128
+
+        @pl.loop(0, self.half // step)
+        def _(i):
+            own = self.partial[aligned(self.base + i * step, step), :].astype(jnp.float32)
+            rows = aligned(i * step, step)
+            total = own + self.pair[rows, :].astype(jnp.float32)
+            self.held[0][rows, :] = total.astype(jnp.bfloat16)
+
+        self.copies = {}
+        self.start_scatter(0)
+
+    def piece(self, level, part, index):
+        start, width, _ = self.parts[part]
+        if level < 2:
+            size = self.held[level].shape[0] // 4
+            return (aligned(index * size, size), pl.ds(start, width))
+        cols = start + lax.rem(index, 2) * (width // 2)
+        return (
+            aligned(lax.div(index, 2) * 16, 16),
+            pl.ds(pl.multiple_of(cols, LANES), width // 2),
+        )
+
+    def landing(self, level, part):
+        start, width, _ = self.parts[part]
+        if level < 2:
+            return (slice(None), pl.ds(start, width))
+        return (slice(None), pl.ds(start // 2, width // 2))
+
+    def start_scatter(self, level):
+        for part, (_, _, order) in enumerate(self.parts):
+            axis = order[level]
+            for k in (1, 2, 3):
+                target = lax.rem(self.near.place(axis) + k, 4)
+                copy = self.copy(
+                    self.held[level].at[self.piece(level, part, target)],
+                    self.incoming[level].at[(k - 1,) + self.landing(level, part)],
+                    1 + (level * len(self.parts) + part) * 3 + k - 1,
+                    self.near.at(axis, k),
+                )
+                copy.start()
+                self.started.append(copy)
+                self.copies[level, part, k] = copy
+
+    def offset(self, part, levels):
+        order = self.parts[part][2]
+        row = self.base
+        for level in range(levels):
+            row = row + self.near.place(order[level]) * (self.half // 4 ** (level + 1))
+        return row
+
+    def final(self, part):
+        start, width, order = self.parts[part]
+        index = self.near.place(order[2])
+        cols = start + lax.rem(index, 2) * (width // 2)
+        rows = self.offset(part, 2) + lax.div(index, 2) * 16
+        return (aligned(rows, 16), pl.ds(pl.multiple_of(cols, LANES), width // 2))
+
+    def scatter(self, level):
+        for part, (_, _, order) in enumerate(self.parts):
+            for k in (1, 2, 3):
+                self.copies[level, part, k].wait_recv()
+            own = self.held[level][self.piece(level, part, self.near.place(order[level]))]
+            total = own.astype(jnp.float32)
+            for k in range(3):
+                total += self.incoming[level][(k,) + self.landing(level, part)].astype(jnp.float32)
+            total = total.astype(jnp.bfloat16)
+            if level < 2:
+                start, width, _ = self.parts[part]
+                self.held[level + 1][:, start : start + width] = total
+            else:
+                self.full[self.final(part)] = total
+        if level < 2:
+            self.start_scatter(level + 1)
+        else:
+            self.start_gather(2)
+
+    def gathered(self, level, part, step):
+        start, width, order = self.parts[part]
+        index = lax.rem(self.near.place(order[level]) + 4 - step, 4)
+        if level == 2:
+            cols = start + lax.rem(index, 2) * (width // 2)
+            rows = self.offset(part, 2) + lax.div(index, 2) * 16
+            return (aligned(rows, 16), pl.ds(pl.multiple_of(cols, LANES), width // 2))
+        size = self.half // 4 ** (level + 1)
+        rows = self.offset(part, level) + index * size
+        return (aligned(rows, size), pl.ds(start, width))
+
+    def start_gather(self, level):
+        for part, (_, _, order) in enumerate(self.parts):
+            for k in (1, 2, 3):
+                slices = self.gathered(level, part, 0)
+                copy = self.copy(
+                    self.full.at[slices],
+                    self.full.at[slices],
+                    1 + ((3 + level) * len(self.parts) + part) * 3 + k - 1,
+                    self.near.at(order[level], k),
+                )
+                copy.start()
+                self.started.append(copy)
+
+    def gather(self, level):
+        for part, (_, _, order) in enumerate(self.parts):
+            for k in (1, 2, 3):
+                slices = self.gathered(level, part, k)
+                self.copy(
+                    self.full.at[slices],
+                    self.full.at[slices],
+                    1 + ((3 + level) * len(self.parts) + part) * 3 + k - 1,
+                    self.near.at(order[level], k),
+                ).wait_recv()
+        if level > 0:
+            self.start_gather(level - 1)
+
+    def gather_pair(self):
+        rows = aligned(self.base, self.half)
+        copy = self.copy(
+            self.full.at[rows], self.full.at[rows], 1 + 18 * len(self.parts), self.near.sibling
+        )
+        copy.start()
+        self.started.append(copy)
+
+    def gather_done(self):
+        rows = aligned((1 - self.near.core) * self.half, self.half)
+        self.copy(
+            self.full.at[rows], self.full.at[rows], 1 + 18 * len(self.parts), self.near.sibling
+        ).wait_recv()
+
+    def sent(self):
+        for copy in self.started:
+            copy.wait_send()
+
+
+def reduction_scratch(parts, width):
+    half = width // 2
+    kind = jnp.bfloat16
+    slots = 2 + 18 * len(parts)
+    return [
+        pltpu.VMEM((width, width), kind),
+        pltpu.VMEM((half, width), kind),
+        pltpu.VMEM((half, width), kind),
+        pltpu.VMEM((3, half // 4, width), kind),
+        pltpu.VMEM((half // 4, width), kind),
+        pltpu.VMEM((3, half // 16, width), kind),
+        pltpu.VMEM((half // 16, width), kind),
+        pltpu.VMEM((3, half // 32, width // 2), kind),
+        pltpu.VMEM((width, width), kind),
+        pltpu.SemaphoreType.DMA((slots,)),
+        pltpu.SemaphoreType.DMA((slots,)),
+    ]
 
 
 def layer_kernel(
@@ -39,13 +265,17 @@
     cross_key,
     cross_value,
     cross_output,
+    encoder_cotangent,
+    decoder_cotangent,
     encoded_out,
     decoded_out,
-    heads_out,
+    own_out,
     cross_out,
     doc,
     states,
     weights,
+    own_cotangent,
+    cross_cotangent,
     normed,
     qkv_send,
     qkv_recv,
@@ -65,6 +295,7 @@
     store_sem,
     send_sem,
     recv_sem,
+    *grad_refs,
 ):
     dp = lax.axis_index("dp")
     me = lax.axis_index("ctx")
@@ -86,19 +317,26 @@
                 (output_weight, weights.at[3]),
                 (cross_key, weights.at[5]),
                 (cross_value, weights.at[6]),
+                (encoder_cotangent, own_cotangent),
                 (cross_output, weights.at[7]),
+                (decoder_cotangent, cross_cotangent),
             ]
         )
     ]
     for load in loads:
         load.start()
 
+    near = Neighbours(dp, me)
     barrier = pltpu.get_barrier_semaphore()
 
     @pl.loop(1, n)
     def _(i):
         peer = lax.rem(me + i, n)
         pl.semaphore_signal(barrier, inc=1, device_id=(dp, peer), device_id_type=MESH)
+
+    others = [near.sibling] + [near.at("x", k) for k in (1, 2, 3)] + [near.at("z", k) for k in (1, 3)]
+    for device in others:
+        pl.semaphore_signal(barrier, inc=1, device_id=device, device_id_type=MESH)
 
     def remote(phase, peer, source, src, dst):
         return pltpu.make_async_remote_copy(
@@ -150,7 +388,7 @@
     normed[...] = norm_rows(doc[...], encoder_gain[...])
     for i in (1, 2, 3):
         loads[i].wait()
-    pl.semaphore_wait(barrier, n - 1)
+    pl.semaphore_wait(barrier, n - 1 + len(others))
 
     @pl.loop(0, blocks)
     def _(i):
@@ -222,19 +460,20 @@
         mixed = matmul(head_recv[...], weights[3, :, wide(i)])
         encoded[:, wide(i)] = (doc[:, wide(i)].astype(jnp.float32) + mixed).astype(jnp.bfloat16)
 
+    own_refs = Reduction(near, OWN_PARTS, *grad_refs[:REFS])
+    cross_refs = Reduction(near, CROSS_PARTS, *grad_refs[REFS:])
     stores = [
         pltpu.make_async_copy(src, dst, store_sem.at[i])
         for i, (src, dst) in enumerate(
             [
                 (encoded, encoded_out),
-                (head_recv, heads_out),
                 (decoded, decoded_out),
-                (cross_recv, cross_out),
+                (own_refs.full, own_out),
+                (cross_refs.full, cross_out),
             ]
         )
     ]
     stores[0].start()
-    stores[1].start()
 
     normed[...] = norm_rows(encoded[...], memory_gain[...])
     loads[7].wait()
@@ -250,6 +489,10 @@
         for half in range(2):
             peer = 2 * block + half
             start(KV, peer, kv_send.at[peer], kv_recv.at[:, me])
+
+    loads[9].wait()
+    own_refs.product(head_recv, own_cotangent)
+    own_refs.pair_sum()
 
     wait_all(SQ, lambda s: sq_send.at[s], lambda s: sq_recv.at[s])
     wait_all(KV, lambda s: kv_send.at[s], lambda s: kv_recv.at[:, s])
@@ -267,29 +510,45 @@
             peer = 2 * pair + half
             start(CROSS, peer, cross_send.at[peer], cross_recv.at[:, column(me)])
 
-    loads[9].wait()
+    own_refs.scatter(0)
+    loads[11].wait()
     wait_all(CROSS, lambda s: cross_send.at[s], lambda s: cross_recv.at[:, column(s)])
+    cross_refs.product(cross_recv, cross_cotangent)
+    loads[10].wait()
 
     @pl.loop(0, blocks)
     def _(i):
         mixed = matmul(cross_recv[...], weights[7, :, wide(i)])
         decoded[:, wide(i)] = (states[:, wide(i)].astype(jnp.float32) + mixed).astype(jnp.bfloat16)
 
+    stores[1].start()
+    cross_refs.pair_sum()
+    own_refs.scatter(1)
+    cross_refs.scatter(0)
+    own_refs.scatter(2)
+    cross_refs.scatter(1)
+    own_refs.gather(2)
+    cross_refs.scatter(2)
+    own_refs.gather(1)
+    cross_refs.gather(2)
+    own_refs.gather(0)
+    cross_refs.gather(1)
+    own_refs.gather_pair()
+    cross_refs.gather(0)
+    own_refs.gather_done()
     stores[2].start()
+    cross_refs.gather_pair()
+    cross_refs.gather_done()
     stores[3].start()
     wait_sent(QKV, lambda p: qkv_send.at[p], lambda p: qkv_recv.at[:, me])
     wait_sent(SQ, lambda p: sq_send.at[p], lambda p: sq_recv.at[me])
     wait_sent(HEAD, lambda p: head_send.at[p], lambda p: head_recv.at[:, column(me)])
     wait_sent(KV, lambda p: kv_send.at[p], lambda p: kv_recv.at[:, me])
     wait_sent(CROSS, lambda p: cross_send.at[p], lambda p: cross_recv.at[:, column(me)])
+    own_refs.sent()
+    cross_refs.sent()
     for store in stores:
         store.wait()
-
-
-def row_products(left, right):
-    return lax.dot_general(
-        left, right, (((0,), (0,)), ((), ())), preferred_element_type=jnp.float32
-    )
 
 
 def solution(mesh):
@@ -317,20 +576,22 @@
         half = jnp.bfloat16
         hbm = pl.BlockSpec(memory_space=pl.ANY)
         vmem = pl.BlockSpec(memory_space=pltpu.VMEM)
-        encoded, decoded, heads, cross_heads = pl.pallas_call(
+        encoded, decoded, own_grad, cross_grad = pl.pallas_call(
             functools.partial(layer_kernel, n),
             out_shape=[
                 jax.ShapeDtypeStruct((rows, width), half),
                 jax.ShapeDtypeStruct((count, width), half),
-                jax.ShapeDtypeStruct((rows, width), half),
-                jax.ShapeDtypeStruct((count, width), half),
+                jax.ShapeDtypeStruct((width, width), half),
+                jax.ShapeDtypeStruct((width, width), half),
             ],
-            in_specs=[hbm] * 2 + [vmem] * 3 + [hbm] * 8,
+            in_specs=[hbm] * 2 + [vmem] * 3 + [hbm] * 10,
             out_specs=[hbm] * 4,
             scratch_shapes=[
                 pltpu.VMEM((rows, width), half),
                 pltpu.VMEM((count, width), half),
                 pltpu.VMEM((8, width, width), half),
+                pltpu.VMEM((rows, width), half),
+                pltpu.VMEM((count, width), half),
                 pltpu.VMEM((rows, width), half),
                 pltpu.VMEM((n, 3, rows, LANES), half),
                 pltpu.VMEM((3, n, rows, LANES), half),
@@ -346,10 +607,12 @@
                 pltpu.VMEM((n * rows, LANES), half),
                 pltpu.VMEM((rows, width), half),
                 pltpu.VMEM((count, width), half),
-                pltpu.SemaphoreType.DMA((10,)),
+                pltpu.SemaphoreType.DMA((12,)),
                 pltpu.SemaphoreType.DMA((4,)),
                 pltpu.SemaphoreType.DMA((5, n)),
                 pltpu.SemaphoreType.DMA((5, n)),
+                *reduction_scratch(OWN_PARTS, width),
+                *reduction_scratch(CROSS_PARTS, width),
             ],
             compiler_params=pltpu.CompilerParams(
                 collective_id=0, has_side_effects=True, vmem_limit_bytes=56 * 2**20
@@ -368,15 +631,14 @@
             cross_key,
             cross_value,
             cross_output,
-        )
-        own_local = row_products(heads, encoder_cotangent[0])
-        cross_local = row_products(cross_heads, decoder_cotangent[0])
-        own_sum, cross_sum = lax.psum((own_local, cross_local), ("dp", "ctx"))
+            encoder_cotangent[0],
+            decoder_cotangent[0],
+        )
         return (
             encoded[None],
             decoded[None],
-            own_sum.astype(jnp.bfloat16),
-            cross_sum.astype(jnp.bfloat16),
+            own_grad,
+            cross_grad,
         )
 
     rows_spec = P("dp", "ctx", None)

time: 195 us -> 131 us (0.67)
  blocking collectives: 114 us -> 0 us
  Pallas kernels: 71.1 us -> 122 us
  local copies, waits for them, and re-layouts: 1.52 us -> 8.09 us
  matrix products: 6.48 us -> 0 us
    psum x1 -> x0, blocking collectives: 114 us -> none  [body(): own_sum, cross_sum = lax.psum((own_local, cross_local), ('dp', 'ctx'))]
    pallas_call x1, Pallas kernels: 71.1 us -> 122 us  [body(): pl.pallas_call(functools.partial(layer_kernel, n), out_shape=[jax.ShapeDt...]
    unnamed x12 -> x6, local copies, waits for them, and re-layouts: 1.52 us -> 8.09 us
    dot_general x2 -> x0, matrix products: 6.48 us -> none  [row_products(): lax.dot_general(left, right, (((0,), (0,)), ((), ())), preferred_element_...]
where the time goes in v2:
time: 131 us
  Pallas kernels  122 us (93%)
  local copies, waits for them, and re-layouts  8.09 us (6%)
    pallas_call x1, Pallas kernels, body(): pl.pallas_call(functools.partial(layer_kernel, n), out_shape=[jax.ShapeDt...  122 us
    unnamed x6, local copies, waits for them, and re-layouts  8.09 us

profile of v2, /device:TPU:1, one launch (start us, length us, event | category | flops | bytes accessed | tf_op | source)
XLA Modules:
  0.0 130.8 jit_solution(8503392158162784156)
XLA Ops:
  0.6 122.1 %shard_map.174 = (bf16[256,1024]{1,0:T(8,128)(2,1)}, bf16[128,1024]{1,0:T(8,128)(2,1)}, bf16[1024,1024]{1,0:T(8,128)(2,1)}, bf16[1024,1024]{1,0:T(8,128)(2,1)}) custom-call(bf16[256,1024]{1,0:T(8,128)(2,1)} %bitcast.9, bf16[128,1024]{1,0:T(8,128)(2,1)} %bitcast.12, f32[1,1024]{1,0:T(1,128)} %bitcast.15, f32[1,1024]{1,0:T(1,128)} %bitcast.16, ...), custom_call_target="tpu_custom_call" | custom-call | tf_op jit(solution)/shard_map/pallas_call | solution.py:579
  122.7 1.9 %copy.23 = bf16[1,256,1024]{2,1,0:T(8,128)(2,1)} copy(bf16[1,256,1024]{2,1,0:T(8,128)(2,1)} %bitcast.11) | data formatting | bytes 1048576
  124.6 1.7 %copy.24 = bf16[1,128,1024]{2,1,0:T(8,128)(2,1)} copy(bf16[1,128,1024]{2,1,0:T(8,128)(2,1)} %bitcast.14) | data formatting | bytes 524288
  126.3 0.0 copy-start
  126.3 3.2 %copy.25 = bf16[1024,1024]{1,0:T(8,128)(2,1)} copy(bf16[1024,1024]{1,0:T(8,128)(2,1)} %get-tuple-element.18) | data formatting | bytes 4194304
  129.5 0.0 copy-done
  129.5 1.3 %copy.26 = bf16[1024,1024]{1,0:T(8,128)(2,1)} copy(bf16[1024,1024]{1,0:T(8,128)(2,1)S(1)} %copy-done) | data formatting | bytes 4194304
Async XLA Ops:
  126.3 3.2 %copy-start = (bf16[1024,1024]{1,0:T(8,128)(2,1)S(1)}, bf16[1024,1024]{1,0:T(8,128)(2,1)}, u32[]{:S(2)}) copy-start(bf16[1024,1024]{1,0:T(8,128)(2,1)} %get-tuple-element.19) | copy-start | bytes 6291460

commit v3 on v1

--- a/solution.py
+++ b/solution.py
@@ -11,7 +11,7 @@
 HEAD_DIM = 64
 LANES = 128
 MESH = pl.DeviceIdType.MESH
-QKV, SQ, HEAD, KV, CROSS = range(5)
+SELF_KV, SELF_Q, SQ, HEAD, KV, CROSS = range(6)
 
 
 def norm_rows(rows, gain):
@@ -22,6 +22,233 @@
 
 def matmul(left, right):
     return jnp.dot(left, right, preferred_element_type=jnp.float32)
+
+
+OWN_PARTS = ((0, 1024, "x"),)
+CROSS_PARTS = ((0, 512, "y"), (512, 512, "z"))
+REFS = 8
+
+
+class Neighbours:
+    def __init__(self, dp, ctx):
+        self.core = lax.rem(dp, 2)
+        self.x = lax.div(dp, 4)
+        self.y = lax.rem(ctx, 4)
+        self.z = lax.div(ctx, 4) * 2 + lax.rem(lax.div(dp, 2), 2)
+        self.sibling = self.device(self.x, self.y, self.z, 1 - self.core)
+
+    def device(self, x, y, z, core):
+        return (x * 4 + lax.rem(z, 2) * 2 + core, lax.div(z, 2) * 4 + y)
+
+    def place(self, axis):
+        return {"x": self.x, "y": self.y, "z": self.z}[axis]
+
+    def step(self, **steps):
+        place = {"x": self.x, "y": self.y, "z": self.z}
+        for axis, step in steps.items():
+            place[axis] = lax.rem(place[axis] + step, 4)
+        return self.device(place["x"], place["y"], place["z"], self.core)
+
+    def distant(self):
+        steps = [(i, j, k) for i in range(4) for j in range(4) for k in range(4)]
+        steps = [(i, j, k) for i, j, k in steps if 0 in (i, j, k) and (i > 0 or k % 2 == 1)]
+        return [self.sibling] + [self.step(x=i, y=j, z=k) for i, j, k in steps]
+
+
+def aligned(start, size):
+    return pl.ds(pl.multiple_of(start, size), size)
+
+
+def grid_of(width):
+    across = min(4, width // LANES)
+    return across, 128 * across // 16, width // across
+
+
+class Reduction:
+    def __init__(
+        self, near, parts, full, partial, pair, first, first_in, second, second_in, send, recv
+    ):
+        self.near = near
+        self.parts = parts
+        self.partial, self.pair, self.full = partial, pair, full
+        self.first, self.first_in = first, first_in
+        self.second, self.second_in = second, second_in
+        self.send, self.recv = send, recv
+        self.half = pair.shape[0]
+        self.base = near.core * self.half
+        self.slot = 0
+        self.started = []
+        self.copies = {}
+
+    def copy(self, key, src, dst, device):
+        slot = len(self.copies)
+        self.copies[key] = pltpu.make_async_remote_copy(
+            src_ref=src,
+            dst_ref=dst,
+            send_sem=self.send.at[slot],
+            recv_sem=self.recv.at[slot],
+            device_id=device,
+            device_id_type=MESH,
+        )
+        self.copies[key].start()
+
+    def arrived(self, key, dst):
+        slot = list(self.copies).index(key)
+        pltpu.make_async_remote_copy(
+            src_ref=dst,
+            dst_ref=dst,
+            send_sem=self.send.at[slot],
+            recv_sem=self.recv.at[slot],
+            device_id=self.near.sibling,
+            device_id_type=MESH,
+        ).wait_recv()
+
+    def product(self, left, right):
+        step = 256
+        for side in (1, 0):
+            start = self.base if side == 0 else (1 - self.near.core) * self.half
+            for i in range(self.half // step):
+                rows = aligned(start + i * step, step)
+                mixed = lax.dot_general(
+                    left[:, rows],
+                    right[...],
+                    (((0,), (0,)), ((), ())),
+                    preferred_element_type=jnp.float32,
+                )
+                self.partial[rows, :] = mixed.astype(jnp.bfloat16)
+                if side == 1:
+                    block = pl.ds(i * step, step)
+                    self.copy(
+                        ("pair", i), self.partial.at[rows], self.pair.at[block], self.near.sibling
+                    )
+
+    def pair_sum(self):
+        step = 256
+        for i in range(self.half // step):
+            block = pl.ds(i * step, step)
+            self.arrived(("pair", i), self.pair.at[block])
+            own = self.partial[aligned(self.base + i * step, step), :].astype(jnp.float32)
+            total = own + self.pair[block, :].astype(jnp.float32)
+            self.first[block, :] = total.astype(jnp.bfloat16)
+        size = self.half // 4
+        for k in (2, 1, 3):
+            for part, (start, width, axis) in enumerate(self.parts):
+                target = lax.rem(self.near.place(axis) + k, 4)
+                cols = pl.ds(start, width)
+                self.copy(
+                    ("first", part, k),
+                    self.first.at[aligned(target * size, size), cols],
+                    self.first_in.at[k - 1, :, cols],
+                    self.near.step(**{axis: k}),
+                )
+
+    def rest(self, part):
+        one, two = [axis for axis in "xyz" if axis != self.parts[part][2]]
+        for i in range(4):
+            for j in range(4):
+                if i or j:
+                    yield i * 4 + j, {one: i, two: j}
+
+    def index(self, part, steps={}):
+        one, two = [axis for axis in "xyz" if axis != self.parts[part][2]]
+        a = lax.rem(self.near.place(one) + steps.get(one, 0), 4)
+        b = lax.rem(self.near.place(two) + steps.get(two, 0), 4)
+        return a * 4 + b
+
+    def piece(self, part, index, base=0):
+        start, width, _ = self.parts[part]
+        across, rows, cols = grid_of(width)
+        row = lax.div(index, across) * rows + base
+        col = start + lax.rem(index, across) * cols
+        return (aligned(row, rows), pl.ds(pl.multiple_of(col, LANES), cols))
+
+    def landing(self, part, k):
+        start, width, _ = self.parts[part]
+        _, rows, cols = grid_of(width)
+        return (k - 1, pl.ds(0, rows), pl.ds(part * LANES, cols))
+
+    def scatter_first(self):
+        size = self.half // 4
+        for part, (start, width, axis) in enumerate(self.parts):
+            cols = pl.ds(start, width)
+            total = self.first[aligned(self.near.place(axis) * size, size), cols].astype(jnp.float32)
+            for k in (1, 3, 2):
+                place = self.first_in.at[k - 1, :, cols]
+                self.arrived(("first", part, k), place)
+                total += place[...].astype(jnp.float32)
+            self.second[:, cols] = total.astype(jnp.bfloat16)
+            for k, steps in self.rest(part):
+                self.copy(
+                    ("second", part, k),
+                    self.second.at[self.piece(part, self.index(part, steps))],
+                    self.second_in.at[self.landing(part, k)],
+                    self.near.step(**steps),
+                )
+
+    def own_rows(self, part, step=0):
+        place = lax.rem(self.near.place(self.parts[part][2]) + 4 - step, 4)
+        return self.base + place * (self.half // 4)
+
+    def scatter_second(self):
+        for part in range(len(self.parts)):
+            total = self.second[self.piece(part, self.index(part))].astype(jnp.float32)
+            for k, _ in self.rest(part):
+                place = self.second_in.at[self.landing(part, k)]
+                self.arrived(("second", part, k), place)
+                total += place[...].astype(jnp.float32)
+            slices = self.piece(part, self.index(part), self.own_rows(part))
+            self.full[slices] = total.astype(jnp.bfloat16)
+            for k, steps in self.rest(part):
+                place = self.full.at[slices]
+                self.copy(("back", part, k), place, place, self.near.step(**steps))
+
+    def gather_second(self):
+        size = self.half // 4
+        for part, (start, width, axis) in enumerate(self.parts):
+            for k, steps in self.rest(part):
+                behind = {name: 4 - step for name, step in steps.items()}
+                slices = self.piece(part, self.index(part, behind), self.own_rows(part))
+                self.arrived(("back", part, k), self.full.at[slices])
+            place = self.full.at[aligned(self.own_rows(part), size), pl.ds(start, width)]
+            for k in (2, 1, 3):
+                self.copy(("last", part, k), place, place, self.near.step(**{axis: k}))
+            self.copy(("across", part, 0), place, place, self.near.sibling)
+
+    def gather_first(self):
+        size = self.half // 4
+        for k in (1, 3, 2):
+            for part, (start, width, axis) in enumerate(self.parts):
+                rows = aligned(self.own_rows(part, k), size)
+                place = self.full.at[rows, pl.ds(start, width)]
+                self.arrived(("last", part, k), place)
+                self.copy(("across", part, k), place, place, self.near.sibling)
+
+    def finish(self):
+        size = self.half // 4
+        for part, (start, width, axis) in enumerate(self.parts):
+            for k in range(4):
+                rows = aligned(
+                    self.own_rows(part, k) + (1 - 2 * self.near.core) * self.half, size
+                )
+                self.arrived(("across", part, k), self.full.at[rows, pl.ds(start, width)])
+        for copy in self.copies.values():
+            copy.wait_send()
+
+
+def reduction_scratch(parts, width):
+    half = width // 2
+    kind = jnp.bfloat16
+    slots = 2 + 40 * len(parts)
+    return [
+        pltpu.VMEM((width, width), kind),
+        pltpu.VMEM((half, width), kind),
+        pltpu.VMEM((half, width), kind),
+        pltpu.VMEM((3, half // 4, width), kind),
+        pltpu.VMEM((half // 4, width), kind),
+        pltpu.VMEM((15, half // 16, width // 2), kind),
+        pltpu.SemaphoreType.DMA((slots,)),
+        pltpu.SemaphoreType.DMA((slots,)),
+    ]
 
 
 def layer_kernel(
@@ -39,13 +266,17 @@
     cross_key,
     cross_value,
     cross_output,
-    encoded_out,
-    decoded_out,
-    heads_out,
-    cross_out,
+    encoder_cotangent,
+    decoder_cotangent,
+    encoded,
+    decoded,
+    own_full,
+    cross_full,
     doc,
     states,
     weights,
+    own_cotangent,
+    cross_cotangent,
     normed,
     qkv_send,
     qkv_recv,
@@ -59,12 +290,10 @@
     cross_recv,
     value_low,
     value_high,
-    encoded,
-    decoded,
     load_sem,
-    store_sem,
     send_sem,
     recv_sem,
+    *grad_refs,
 ):
     dp = lax.axis_index("dp")
     me = lax.axis_index("ctx")
@@ -86,19 +315,26 @@
                 (output_weight, weights.at[3]),
                 (cross_key, weights.at[5]),
                 (cross_value, weights.at[6]),
+                (encoder_cotangent, own_cotangent),
                 (cross_output, weights.at[7]),
+                (decoder_cotangent, cross_cotangent),
             ]
         )
     ]
-    for load in loads:
-        load.start()
-
+    for i in (0, 2, 3, 1, 4, 5, 6, 7, 8, 9, 10, 11):
+        loads[i].start()
+
+    near = Neighbours(dp, me)
     barrier = pltpu.get_barrier_semaphore()
 
     @pl.loop(1, n)
     def _(i):
         peer = lax.rem(me + i, n)
         pl.semaphore_signal(barrier, inc=1, device_id=(dp, peer), device_id_type=MESH)
+
+    others = near.distant()
+    for device in others:
+        pl.semaphore_signal(barrier, inc=1, device_id=device, device_id_type=MESH)
 
     def remote(phase, peer, source, src, dst):
         return pltpu.make_async_remote_copy(
@@ -122,16 +358,19 @@
         def _():
             local(phase, src, dst).start()
 
+    def wait_one(phase, source, src, dst):
+        @pl.when(source != me)
+        def _():
+            remote(phase, source, source, src, dst).wait_recv()
+
+        @pl.when(source == me)
+        def _():
+            local(phase, src, dst).wait()
+
     def wait_all(phase, src_of, dst_of):
         @pl.loop(0, n)
         def _(source):
-            @pl.when(source != me)
-            def _():
-                remote(phase, source, source, src_of(source), dst_of(source)).wait_recv()
-
-            @pl.when(source == me)
-            def _():
-                local(phase, src_of(source), dst_of(source)).wait()
+            wait_one(phase, source, src_of(source), dst_of(source))
 
     def wait_sent(phase, src_of, dst_of):
         @pl.loop(0, n)
@@ -148,20 +387,28 @@
 
     loads[0].wait()
     normed[...] = norm_rows(doc[...], encoder_gain[...])
-    for i in (1, 2, 3):
-        loads[i].wait()
-    pl.semaphore_wait(barrier, n - 1)
+    pl.semaphore_wait(barrier, n - 1 + len(others))
+    loads[2].wait()
+    loads[3].wait()
 
     @pl.loop(0, blocks)
     def _(i):
         block = lax.rem(lax.div(me, 2) + (blocks - 1) - i, blocks)
-        for t in range(3):
+        for t in (1, 2):
             part = matmul(normed[...], weights[t, :, wide(block)]).astype(jnp.bfloat16)
             qkv_send[2 * block, t] = part[:, :LANES]
             qkv_send[2 * block + 1, t] = part[:, LANES:]
         for half in range(2):
             peer = 2 * block + half
-            start(QKV, peer, qkv_send.at[peer], qkv_recv.at[:, me])
+            start(SELF_KV, peer, qkv_send.at[peer, pl.ds(1, 2)], qkv_recv.at[pl.ds(1, 2), me])
+
+    loads[1].wait()
+
+    @pl.loop(0, blocks)
+    def _(i):
+        part = matmul(normed[...], weights[0, :, wide(i)]).astype(jnp.bfloat16)
+        qkv_send[2 * i, 0] = part[:, :LANES]
+        qkv_send[2 * i + 1, 0] = part[:, LANES:]
 
     loads[4].wait()
     loads[5].wait()
@@ -169,13 +416,17 @@
 
     @pl.loop(0, blocks)
     def _(i):
-        block = lax.rem(lax.div(me, 2) + (blocks - 1) - i, blocks)
-        part = matmul(normed[0:count, :], weights[4, :, wide(block)]).astype(jnp.bfloat16)
-        sq_send[2 * block] = part[:, :LANES]
-        sq_send[2 * block + 1] = part[:, LANES:]
-        for half in range(2):
-            peer = 2 * block + half
-            start(SQ, peer, sq_send.at[peer], sq_recv.at[me])
+        part = matmul(normed[0:count, :], weights[4, :, wide(i)]).astype(jnp.bfloat16)
+        sq_send[2 * i] = part[:, :LANES]
+        sq_send[2 * i + 1] = part[:, LANES:]
+
+    kv_sent = lambda p: qkv_send.at[p, pl.ds(1, 2)], lambda p: qkv_recv.at[pl.ds(1, 2), me]
+    wait_sent(SELF_KV, *kv_sent)
+
+    @pl.loop(0, n)
+    def _(i):
+        peer = lax.rem(me + n - i, n)
+        start(SELF_Q, peer, qkv_send.at[peer, 0], qkv_recv.at[0, me])
 
     lane = lax.broadcasted_iota(jnp.int32, (1, LANES), 1)
     low = lane < HEAD_DIM
@@ -204,16 +455,25 @@
         )
         return (mixed / total).astype(jnp.bfloat16)
 
-    wait_all(QKV, lambda s: qkv_send.at[s], lambda s: qkv_recv.at[:, s])
+    wait_all(
+        SELF_KV, lambda s: qkv_send.at[s, pl.ds(1, 2)], lambda s: qkv_recv.at[pl.ds(1, 2), s]
+    )
     set_values(qkv_recv.at[2])
 
     @pl.loop(0, n)
     def _(i):
-        peer = lax.rem(me + 1 + i, n)
+        peer = lax.rem(me + i, n)
+        wait_one(SELF_Q, peer, qkv_send.at[peer, 0], qkv_recv.at[0, peer])
         keys = qkv_recv[1].reshape(n * rows, LANES)
         head_send[peer] = attend(qkv_recv[0, peer], keys)
         start(HEAD, peer, head_send.at[peer], head_recv.at[:, column(me)])
 
+        @pl.when(i == 2)
+        def _():
+            @pl.loop(0, n)
+            def _(p):
+                start(SQ, p, sq_send.at[p], sq_recv.at[me])
+
     loads[6].wait()
     wait_all(HEAD, lambda s: head_send.at[s], lambda s: head_recv.at[:, column(s)])
 
@@ -222,19 +482,8 @@
         mixed = matmul(head_recv[...], weights[3, :, wide(i)])
         encoded[:, wide(i)] = (doc[:, wide(i)].astype(jnp.float32) + mixed).astype(jnp.bfloat16)
 
-    stores = [
-        pltpu.make_async_copy(src, dst, store_sem.at[i])
-        for i, (src, dst) in enumerate(
-            [
-                (encoded, encoded_out),
-                (head_recv, heads_out),
-                (decoded, decoded_out),
-                (cross_recv, cross_out),
-            ]
-        )
-    ]
-    stores[0].start()
-    stores[1].start()
+    own_refs = Reduction(near, OWN_PARTS, own_full, *grad_refs[:REFS])
+    cross_refs = Reduction(near, CROSS_PARTS, cross_full, *grad_refs[REFS:])
 
     normed[...] = norm_rows(encoded[...], memory_gain[...])
     loads[7].wait()
@@ -250,6 +499,10 @@
         for half in range(2):
             peer = 2 * block + half
             start(KV, peer, kv_send.at[peer], kv_recv.at[:, me])
+
+    loads[9].wait()
+    own_refs.product(head_recv, own_cotangent)
+    own_refs.pair_sum()
 
     wait_all(SQ, lambda s: sq_send.at[s], lambda s: sq_recv.at[s])
     wait_all(KV, lambda s: kv_send.at[s], lambda s: kv_recv.at[:, s])
@@ -267,29 +520,32 @@
             peer = 2 * pair + half
             start(CROSS, peer, cross_send.at[peer], cross_recv.at[:, column(me)])
 
-    loads[9].wait()
+    loads[11].wait()
     wait_all(CROSS, lambda s: cross_send.at[s], lambda s: cross_recv.at[:, column(s)])
+    cross_refs.product(cross_recv, cross_cotangent)
+    own_refs.scatter_first()
+    cross_refs.pair_sum()
+    loads[10].wait()
 
     @pl.loop(0, blocks)
     def _(i):
         mixed = matmul(cross_recv[...], weights[7, :, wide(i)])
         decoded[:, wide(i)] = (states[:, wide(i)].astype(jnp.float32) + mixed).astype(jnp.bfloat16)
 
-    stores[2].start()
-    stores[3].start()
-    wait_sent(QKV, lambda p: qkv_send.at[p], lambda p: qkv_recv.at[:, me])
+    own_refs.scatter_second()
+    cross_refs.scatter_first()
+    own_refs.gather_second()
+    cross_refs.scatter_second()
+    cross_refs.gather_second()
+    own_refs.gather_first()
+    cross_refs.gather_first()
+    own_refs.finish()
+    cross_refs.finish()
+    wait_sent(SELF_Q, lambda p: qkv_send.at[p, 0], lambda p: qkv_recv.at[0, me])
     wait_sent(SQ, lambda p: sq_send.at[p], lambda p: sq_recv.at[me])
     wait_sent(HEAD, lambda p: head_send.at[p], lambda p: head_recv.at[:, column(me)])
     wait_sent(KV, lambda p: kv_send.at[p], lambda p: kv_recv.at[:, me])
     wait_sent(CROSS, lambda p: cross_send.at[p], lambda p: cross_recv.at[:, column(me)])
-    for store in stores:
-        store.wait()
-
-
-def row_products(left, right):
-    return lax.dot_general(
-        left, right, (((0,), (0,)), ((), ())), preferred_element_type=jnp.float32
-    )
 
 
 def solution(mesh):
@@ -317,20 +573,18 @@
         half = jnp.bfloat16
         hbm = pl.BlockSpec(memory_space=pl.ANY)
         vmem = pl.BlockSpec(memory_space=pltpu.VMEM)
-        encoded, decoded, heads, cross_heads = pl.pallas_call(
+        shapes = [(rows, width), (count, width), (width, width), (width, width)]
+        encoded, decoded, own_grad, cross_grad = pl.pallas_call(
             functools.partial(layer_kernel, n),
-            out_shape=[
-                jax.ShapeDtypeStruct((rows, width), half),
-                jax.ShapeDtypeStruct((count, width), half),
-                jax.ShapeDtypeStruct((rows, width), half),
-                jax.ShapeDtypeStruct((count, width), half),
-            ],
-            in_specs=[hbm] * 2 + [vmem] * 3 + [hbm] * 8,
-            out_specs=[hbm] * 4,
+            out_shape=[pltpu.VMEM(shape, half) for shape in shapes],
+            in_specs=[hbm] * 2 + [vmem] * 3 + [hbm] * 10,
+            out_specs=[vmem] * 4,
             scratch_shapes=[
                 pltpu.VMEM((rows, width), half),
                 pltpu.VMEM((count, width), half),
                 pltpu.VMEM((8, width, width), half),
+                pltpu.VMEM((rows, width), half),
+                pltpu.VMEM((count, width), half),
                 pltpu.VMEM((rows, width), half),
                 pltpu.VMEM((n, 3, rows, LANES), half),
                 pltpu.VMEM((3, n, rows, LANES), half),
@@ -344,15 +598,14 @@
                 pltpu.VMEM((count, width), half),
                 pltpu.VMEM((n * rows, LANES), half),
                 pltpu.VMEM((n * rows, LANES), half),
-                pltpu.VMEM((rows, width), half),
-                pltpu.VMEM((count, width), half),
-                pltpu.SemaphoreType.DMA((10,)),
-                pltpu.SemaphoreType.DMA((4,)),
-                pltpu.SemaphoreType.DMA((5, n)),
-                pltpu.SemaphoreType.DMA((5, n)),
+                pltpu.SemaphoreType.DMA((12,)),
+                pltpu.SemaphoreType.DMA((6, n)),
+                pltpu.SemaphoreType.DMA((6, n)),
+                *reduction_scratch(OWN_PARTS, width),
+                *reduction_scratch(CROSS_PARTS, width),
             ],
             compiler_params=pltpu.CompilerParams(
-                collective_id=0, has_side_effects=True, vmem_limit_bytes=56 * 2**20
+                collective_id=0, has_side_effects=True, vmem_limit_bytes=50 * 2**20
             ),
         )(
             document[0],
@@ -368,15 +621,14 @@
             cross_key,
             cross_value,
             cross_output,
+            encoder_cotangent[0],
+            decoder_cotangent[0],
         )
-        own_local = row_products(heads, encoder_cotangent[0])
-        cross_local = row_products(cross_heads, decoder_cotangent[0])
-        own_sum, cross_sum = lax.psum((own_local, cross_local), ("dp", "ctx"))
         return (
             encoded[None],
             decoded[None],
-            own_sum.astype(jnp.bfloat16),
-            cross_sum.astype(jnp.bfloat16),
+            own_grad,
+            cross_grad,
         )
 
     rows_spec = P("dp", "ctx", None)

time: 195 us -> 120 us (0.62)
  blocking collectives: 114 us -> 0 us
  Pallas kernels: 71.1 us -> 115 us
  matrix products: 6.48 us -> 0 us
  local copies, waits for them, and re-layouts: 1.52 us -> 4.13 us
    psum x1 -> x0, blocking collectives: 114 us -> none  [body(): own_sum, cross_sum = lax.psum((own_local, cross_local), ('dp', 'ctx'))]
    pallas_call x1, Pallas kernels: 71.1 us -> 115 us  [body(): pl.pallas_call(functools.partial(layer_kernel, n), out_shape=[pltpu.VMEM(...]
    dot_general x2 -> x0, matrix products: 6.48 us -> none  [row_products(): lax.dot_general(left, right, (((0,), (0,)), ((), ())), preferred_element_...]
    unnamed x12 -> x4, local copies, waits for them, and re-layouts: 1.52 us -> 4.13 us
where the time goes in v3:
time: 120 us
  Pallas kernels  115 us (96%)
  local copies, waits for them, and re-layouts  4.13 us (3%)
    pallas_call x1, Pallas kernels, body(): pl.pallas_call(functools.partial(layer_kernel, n), out_shape=[pltpu.VMEM(...  115 us
    unnamed x4, local copies, waits for them, and re-layouts  4.13 us

profile of v3, /device:TPU:1, one launch (start us, length us, event | category | flops | bytes accessed | tf_op | source)
XLA Modules:
  0.0 119.6 jit_solution(2637777827547535580)
XLA Ops:
  0.6 114.8 %shard_map.174 = (bf16[256,1024]{1,0:T(8,128)(2,1)S(1)}, bf16[128,1024]{1,0:T(8,128)(2,1)S(1)}, bf16[1024,1024]{1,0:T(8,128)(2,1)S(1)}, bf16[1024,1024]{1,0:T(8,128)(2,1)S(1)}) custom-call(bf16[256,1024]{1,0:T(8,128)(2,1)} %bitcast.11, bf16[128,1024]{1,0:T(8,128)(2,1)} %bitcast.13, f32[1,1024]{1,0:T(1,128)} %bitcast.15, f32[1,1024]{1,0:T(1,128)} %bitcast.16, ...), custom_call_target="tpu_custom_call" | custom-call | tf_op jit(solution)/shard_map/pallas_call | solution.py:577
  115.4 0.8 copy.23
  116.2 0.7 copy.24
  116.9 1.3 %copy.25 = bf16[1024,1024]{1,0:T(8,128)(2,1)} copy(bf16[1024,1024]{1,0:T(8,128)(2,1)S(1)} %get-tuple-element.14) | data formatting | bytes 4194304
  118.2 1.3 %copy.26 = bf16[1024,1024]{1,0:T(8,128)(2,1)} copy(bf16[1024,1024]{1,0:T(8,128)(2,1)S(1)} %get-tuple-element.15) | data formatting | bytes 4194304

commit v4 on v3

--- a/solution.py
+++ b/solution.py
@@ -25,43 +25,41 @@
 
 
 OWN_PARTS = ((0, 1024, "x"),)
-CROSS_PARTS = ((0, 512, "y"), (512, 512, "z"))
+CROSS_PARTS = ((0, 512, "y"), (512, 256, "z"), (768, 256, "x"))
 REFS = 8
 
 
 class Neighbours:
     def __init__(self, dp, ctx):
-        self.core = lax.rem(dp, 2)
-        self.x = lax.div(dp, 4)
-        self.y = lax.rem(ctx, 4)
-        self.z = lax.div(ctx, 4) * 2 + lax.rem(lax.div(dp, 2), 2)
-        self.sibling = self.device(self.x, self.y, self.z, 1 - self.core)
-
-    def device(self, x, y, z, core):
-        return (x * 4 + lax.rem(z, 2) * 2 + core, lax.div(z, 2) * 4 + y)
-
-    def place(self, axis):
-        return {"x": self.x, "y": self.y, "z": self.z}[axis]
-
-    def step(self, **steps):
-        place = {"x": self.x, "y": self.y, "z": self.z}
-        for axis, step in steps.items():
-            place[axis] = lax.rem(place[axis] + step, 4)
-        return self.device(place["x"], place["y"], place["z"], self.core)
+        self.core = dp & 1
+        low, high = (dp >> 1) & 1, ctx >> 2
+        place = {"x": dp >> 2, "y": ctx & 3, "z": high * 2 + low}
+        self.places = {axis: [(start + k) & 3 for k in range(4)] for axis, start in place.items()}
+        self.dp_x = [x * 4 for x in self.places["x"]]
+        self.dp_z = [(z & 1) * 2 + self.core for z in self.places["z"]]
+        self.ctx_z = [(z >> 1) * 4 for z in self.places["z"]]
+        self.sibling = (dp + 1 - 2 * self.core, ctx)
+
+    def step(self, x=0, y=0, z=0):
+        return (self.dp_x[x] + self.dp_z[z], self.ctx_z[z] + self.places["y"][y])
 
     def distant(self):
-        steps = [(i, j, k) for i in range(4) for j in range(4) for k in range(4)]
-        steps = [(i, j, k) for i, j, k in steps if 0 in (i, j, k) and (i > 0 or k % 2 == 1)]
-        return [self.sibling] + [self.step(x=i, y=j, z=k) for i, j, k in steps]
+        parts = OWN_PARTS + CROSS_PARTS
+        reached = {tuple(k if axis == name else 0 for name in "xyz") for *_, axis in parts for k in (1, 2, 3)}
+        for *_, axis in parts:
+            for steps in rest(axis):
+                reached.add(tuple(steps.get(name, 0) for name in "xyz"))
+        reached = sorted((i, j, k) for i, j, k in reached if i > 0 or k % 2 == 1)
+        return [self.sibling] + [self.step(*steps) for steps in reached]
+
+
+def rest(axis):
+    one, two = [name for name in "xyz" if name != axis]
+    return [{one: i, two: j} for i in range(4) for j in range(4) if i or j]
 
 
 def aligned(start, size):
     return pl.ds(pl.multiple_of(start, size), size)
-
-
-def grid_of(width):
-    across = min(4, width // LANES)
-    return across, 128 * across // 16, width // across
 
 
 class Reduction:
@@ -75,14 +73,14 @@
         self.second, self.second_in = second, second_in
         self.send, self.recv = send, recv
         self.half = pair.shape[0]
+        self.size = self.half // 4
         self.base = near.core * self.half
-        self.slot = 0
-        self.started = []
-        self.copies = {}
+        self.other = self.half - self.base
+        self.slots = {}
 
     def copy(self, key, src, dst, device):
-        slot = len(self.copies)
-        self.copies[key] = pltpu.make_async_remote_copy(
+        slot = self.slots.setdefault(key, len(self.slots))
+        return pltpu.make_async_remote_copy(
             src_ref=src,
             dst_ref=dst,
             send_sem=self.send.at[slot],
@@ -90,23 +88,17 @@
             device_id=device,
             device_id_type=MESH,
         )
-        self.copies[key].start()
-
-    def arrived(self, key, dst):
-        slot = list(self.copies).index(key)
-        pltpu.make_async_remote_copy(
-            src_ref=dst,
-            dst_ref=dst,
-            send_sem=self.send.at[slot],
-            recv_sem=self.recv.at[slot],
-            device_id=self.near.sibling,
-            device_id_type=MESH,
-        ).wait_recv()
+
+    def arrived(self, key, place):
+        self.copy(key, place, place, self.near.sibling).wait_recv()
+
+    def left(self, key, place):
+        self.copy(key, place, place, self.near.sibling).wait_send()
 
     def product(self, left, right):
         step = 256
         for side in (1, 0):
-            start = self.base if side == 0 else (1 - self.near.core) * self.half
+            start = self.base if side == 0 else self.other
             for i in range(self.half // step):
                 rows = aligned(start + i * step, step)
                 mixed = lax.dot_general(
@@ -120,7 +112,10 @@
                     block = pl.ds(i * step, step)
                     self.copy(
                         ("pair", i), self.partial.at[rows], self.pair.at[block], self.near.sibling
-                    )
+                    ).start()
+
+    def place(self, axis, k=0):
+        return self.near.places[axis][k]
 
     def pair_sum(self):
         step = 256
@@ -130,122 +125,108 @@
             own = self.partial[aligned(self.base + i * step, step), :].astype(jnp.float32)
             total = own + self.pair[block, :].astype(jnp.float32)
             self.first[block, :] = total.astype(jnp.bfloat16)
-        size = self.half // 4
         for k in (2, 1, 3):
             for part, (start, width, axis) in enumerate(self.parts):
-                target = lax.rem(self.near.place(axis) + k, 4)
                 cols = pl.ds(start, width)
                 self.copy(
-                    ("first", part, k),
-                    self.first.at[aligned(target * size, size), cols],
+                    ("first", part),
+                    self.first.at[aligned(self.place(axis, k) * self.size, self.size), cols],
                     self.first_in.at[k - 1, :, cols],
                     self.near.step(**{axis: k}),
-                )
-
-    def rest(self, part):
-        one, two = [axis for axis in "xyz" if axis != self.parts[part][2]]
-        for i in range(4):
-            for j in range(4):
-                if i or j:
-                    yield i * 4 + j, {one: i, two: j}
-
-    def index(self, part, steps={}):
-        one, two = [axis for axis in "xyz" if axis != self.parts[part][2]]
-        a = lax.rem(self.near.place(one) + steps.get(one, 0), 4)
-        b = lax.rem(self.near.place(two) + steps.get(two, 0), 4)
-        return a * 4 + b
-
-    def piece(self, part, index, base=0):
+                ).start()
+
+    def piece(self, part, steps, base=0):
+        start, width, axis = self.parts[part]
+        one, two = [name for name in "xyz" if name != axis]
+        first, second = self.place(one, steps.get(one, 0)), self.place(two, steps.get(two, 0))
+        row = (first * 2 + (second >> 1)) * 16 + base
+        col = (second & 1) * (width // 2) + start
+        return (aligned(row, 16), pl.ds(pl.multiple_of(col, LANES), width // 2))
+
+    def landing(self, part):
         start, width, _ = self.parts[part]
-        across, rows, cols = grid_of(width)
-        row = lax.div(index, across) * rows + base
-        col = start + lax.rem(index, across) * cols
-        return (aligned(row, rows), pl.ds(pl.multiple_of(col, LANES), cols))
-
-    def landing(self, part, k):
-        start, width, _ = self.parts[part]
-        _, rows, cols = grid_of(width)
-        return (k - 1, pl.ds(0, rows), pl.ds(part * LANES, cols))
+        return pl.ds(start // 2, width // 2)
 
     def scatter_first(self):
-        size = self.half // 4
         for part, (start, width, axis) in enumerate(self.parts):
             cols = pl.ds(start, width)
-            total = self.first[aligned(self.near.place(axis) * size, size), cols].astype(jnp.float32)
-            for k in (1, 3, 2):
-                place = self.first_in.at[k - 1, :, cols]
-                self.arrived(("first", part, k), place)
-                total += place[...].astype(jnp.float32)
+            self.arrived(("first", part), self.first_in.at[:, :, cols])
+            total = self.first[aligned(self.place(axis) * self.size, self.size), cols].astype(jnp.float32)
+            for k in range(3):
+                total += self.first_in[k, :, cols].astype(jnp.float32)
             self.second[:, cols] = total.astype(jnp.bfloat16)
-            for k, steps in self.rest(part):
+            for k, steps in enumerate(rest(axis)):
                 self.copy(
-                    ("second", part, k),
-                    self.second.at[self.piece(part, self.index(part, steps))],
-                    self.second_in.at[self.landing(part, k)],
+                    ("second", part),
+                    self.second.at[self.piece(part, steps)],
+                    self.second_in.at[k, :, self.landing(part)],
                     self.near.step(**steps),
-                )
-
-    def own_rows(self, part, step=0):
-        place = lax.rem(self.near.place(self.parts[part][2]) + 4 - step, 4)
-        return self.base + place * (self.half // 4)
+                ).start()
+
+    def own_rows(self, part, k=0):
+        return self.base + self.place(self.parts[part][2], k) * self.size
 
     def scatter_second(self):
-        for part in range(len(self.parts)):
-            total = self.second[self.piece(part, self.index(part))].astype(jnp.float32)
-            for k, _ in self.rest(part):
-                place = self.second_in.at[self.landing(part, k)]
-                self.arrived(("second", part, k), place)
-                total += place[...].astype(jnp.float32)
-            slices = self.piece(part, self.index(part), self.own_rows(part))
+        for part, (start, width, axis) in enumerate(self.parts):
+            cols = self.landing(part)
+            self.arrived(("second", part), self.second_in.at[:, :, cols])
+            total = self.second[self.piece(part, {})].astype(jnp.float32)
+            for k in range(15):
+                total += self.second_in[k, :, cols].astype(jnp.float32)
+            slices = self.piece(part, {}, self.own_rows(part))
             self.full[slices] = total.astype(jnp.bfloat16)
-            for k, steps in self.rest(part):
-                place = self.full.at[slices]
-                self.copy(("back", part, k), place, place, self.near.step(**steps))
+            place = self.full.at[slices]
+            for steps in rest(axis):
+                self.copy(("back", part), place, place, self.near.step(**steps)).start()
 
     def gather_second(self):
-        size = self.half // 4
         for part, (start, width, axis) in enumerate(self.parts):
-            for k, steps in self.rest(part):
-                behind = {name: 4 - step for name, step in steps.items()}
-                slices = self.piece(part, self.index(part, behind), self.own_rows(part))
-                self.arrived(("back", part, k), self.full.at[slices])
-            place = self.full.at[aligned(self.own_rows(part), size), pl.ds(start, width)]
+            cols = pl.ds(start, width)
+            self.arrived(("back", part), self.second_in.at[:, :, self.landing(part)])
+            place = self.full.at[aligned(self.own_rows(part), self.size), cols]
             for k in (2, 1, 3):
-                self.copy(("last", part, k), place, place, self.near.step(**{axis: k}))
-            self.copy(("across", part, 0), place, place, self.near.sibling)
+                self.copy(("last", part, 4 - k), place, place, self.near.step(**{axis: k})).start()
+            self.copy(("across", part, 0), place, place, self.near.sibling).start()
 
     def gather_first(self):
-        size = self.half // 4
         for k in (1, 3, 2):
             for part, (start, width, axis) in enumerate(self.parts):
-                rows = aligned(self.own_rows(part, k), size)
-                place = self.full.at[rows, pl.ds(start, width)]
+                place = self.full.at[aligned(self.own_rows(part, k), self.size), pl.ds(start, width)]
                 self.arrived(("last", part, k), place)
-                self.copy(("across", part, k), place, place, self.near.sibling)
+                self.copy(("across", part, k), place, place, self.near.sibling).start()
 
     def finish(self):
-        size = self.half // 4
+        turn = self.other - self.base
         for part, (start, width, axis) in enumerate(self.parts):
+            cols = pl.ds(start, width)
             for k in range(4):
-                rows = aligned(
-                    self.own_rows(part, k) + (1 - 2 * self.near.core) * self.half, size
-                )
-                self.arrived(("across", part, k), self.full.at[rows, pl.ds(start, width)])
-        for copy in self.copies.values():
-            copy.wait_send()
+                rows = aligned(self.own_rows(part, k) + turn, self.size)
+                self.arrived(("across", part, k), self.full.at[rows, cols])
+        for part, (start, width, axis) in enumerate(self.parts):
+            cols = pl.ds(start, width)
+            self.left(("first", part), self.first_in.at[:, :, cols])
+            self.left(("second", part), self.second_in.at[:, :, self.landing(part)])
+            self.left(("back", part), self.second_in.at[:, :, self.landing(part)])
+            block = self.full.at[pl.ds(0, self.size), cols]
+            for k in (1, 2, 3):
+                self.left(("last", part, k), block)
+            for k in range(4):
+                self.left(("across", part, k), block)
+        for i in range(self.half // 256):
+            self.left(("pair", i), self.pair.at[pl.ds(i * 256, 256)])
 
 
 def reduction_scratch(parts, width):
     half = width // 2
     kind = jnp.bfloat16
-    slots = 2 + 40 * len(parts)
+    slots = 2 + 10 * len(parts)
     return [
         pltpu.VMEM((width, width), kind),
         pltpu.VMEM((half, width), kind),
         pltpu.VMEM((half, width), kind),
         pltpu.VMEM((3, half // 4, width), kind),
         pltpu.VMEM((half // 4, width), kind),
-        pltpu.VMEM((15, half // 16, width // 2), kind),
+        pltpu.VMEM((15, half // 32, width // 2), kind),
         pltpu.SemaphoreType.DMA((slots,)),
         pltpu.SemaphoreType.DMA((slots,)),
     ]
@@ -321,7 +302,7 @@
             ]
         )
     ]
-    for i in (0, 2, 3, 1, 4, 5, 6, 7, 8, 9, 10, 11):
+    for i in (0, 2, 3):
         loads[i].start()
 
     near = Neighbours(dp, me)
@@ -390,6 +371,8 @@
     pl.semaphore_wait(barrier, n - 1 + len(others))
     loads[2].wait()
     loads[3].wait()
+    for i in (1, 4, 5, 6, 7, 8, 9, 10, 11):
+        loads[i].start()
 
     @pl.loop(0, blocks)
     def _(i):
@@ -508,8 +491,7 @@
     wait_all(KV, lambda s: kv_send.at[s], lambda s: kv_recv.at[:, s])
     set_values(kv_recv.at[1])
 
-    @pl.loop(0, n // 2)
-    def _(i):
+    def cross_block(i):
         pair = lax.rem(lax.div(me, 2) + 1 + i, n // 2)
         keys = kv_recv[0].reshape(n * rows, LANES)
         query = sq_recv[pl.ds(2 * pair, 2)].reshape(2 * count, LANES)
@@ -520,10 +502,13 @@
             peer = 2 * pair + half
             start(CROSS, peer, cross_send.at[peer], cross_recv.at[:, column(me)])
 
+    pl.loop(0, n // 2 - 1)(cross_block)
+    own_refs.scatter_first()
+    cross_block(n // 2 - 1)
     loads[11].wait()
     wait_all(CROSS, lambda s: cross_send.at[s], lambda s: cross_recv.at[:, column(s)])
     cross_refs.product(cross_recv, cross_cotangent)
-    own_refs.scatter_first()
+    own_refs.scatter_second()
     cross_refs.pair_sum()
     loads[10].wait()
 
@@ -532,12 +517,11 @@
         mixed = matmul(cross_recv[...], weights[7, :, wide(i)])
         decoded[:, wide(i)] = (states[:, wide(i)].astype(jnp.float32) + mixed).astype(jnp.bfloat16)
 
-    own_refs.scatter_second()
+    own_refs.gather_second()
     cross_refs.scatter_first()
-    own_refs.gather_second()
     cross_refs.scatter_second()
+    own_refs.gather_first()
     cross_refs.gather_second()
-    own_refs.gather_first()
     cross_refs.gather_first()
     own_refs.finish()
     cross_refs.finish()

time: 120 us -> 114 us (0.950)
  Pallas kernels: 115 us -> 109 us
    pallas_call x1, Pallas kernels: 115 us -> 109 us  [body(): pl.pallas_call(functools.partial(layer_kernel, n), out_shape=[pltpu.VMEM(...]
where the time goes in v4:
time: 114 us; the launch traced here: 113 us
  Pallas kernels  109 us (96%)
  local copies, waits for them, and re-layouts  4.13 us (4%)
    pallas_call x1, Pallas kernels, body(): pl.pallas_call(functools.partial(layer_kernel, n), out_shape=[pltpu.VMEM(...  109 us
    unnamed x4, local copies, waits for them, and re-layouts  4.13 us

profile of v4, /device:TPU:1, one launch (start us, length us, event | category | flops | bytes accessed | tf_op | source)
XLA Modules:
  0.0 113.4 jit_solution(5900476610941033640)
XLA Ops:
  0.6 108.6 %shard_map.174 = (bf16[256,1024]{1,0:T(8,128)(2,1)S(1)}, bf16[128,1024]{1,0:T(8,128)(2,1)S(1)}, bf16[1024,1024]{1,0:T(8,128)(2,1)S(1)}, bf16[1024,1024]{1,0:T(8,128)(2,1)S(1)}) custom-call(bf16[256,1024]{1,0:T(8,128)(2,1)} %bitcast.11, bf16[128,1024]{1,0:T(8,128)(2,1)} %bitcast.13, f32[1,1024]{1,0:T(1,128)} %bitcast.15, f32[1,1024]{1,0:T(1,128)} %bitcast.16, ...), custom_call_target="tpu_custom_call" | custom-call | tf_op jit(solution)/shard_map/pallas_call | solution.py:561
  109.2 0.8 copy.23
  110.0 0.7 copy.24
  110.7 1.3 %copy.25 = bf16[1024,1024]{1,0:T(8,128)(2,1)} copy(bf16[1024,1024]{1,0:T(8,128)(2,1)S(1)} %get-tuple-element.14) | data formatting | bytes 4194304
  112.1 1.3 %copy.26 = bf16[1024,1024]{1,0:T(8,128)(2,1)} copy(bf16[1024,1024]{1,0:T(8,128)(2,1)S(1)} %get-tuple-element.15) | data formatting | bytes 4194304

commit v5 on v4

--- a/solution.py
+++ b/solution.py
@@ -11,7 +11,7 @@
 HEAD_DIM = 64
 LANES = 128
 MESH = pl.DeviceIdType.MESH
-SELF_KV, SELF_Q, SQ, HEAD, KV, CROSS = range(6)
+SELF_KV, SELF_Q, SQ, HEAD, KV, KV_LATE, CROSS = range(7)
 
 
 def norm_rows(rows, gain):
@@ -24,7 +24,7 @@
     return jnp.dot(left, right, preferred_element_type=jnp.float32)
 
 
-OWN_PARTS = ((0, 1024, "x"),)
+OWN_PARTS = ((0, 512, "x"), (512, 256, "y"), (768, 256, "z"))
 CROSS_PARTS = ((0, 512, "y"), (512, 256, "z"), (768, 256, "x"))
 REFS = 8
 
@@ -267,6 +267,7 @@
     head_recv,
     kv_send,
     kv_recv,
+    early,
     cross_send,
     cross_recv,
     value_low,
@@ -421,21 +422,25 @@
         value_low[...] = jnp.where(low, values, one)
         value_high[...] = jnp.where(low, one, values)
 
-    def attend(query, keys):
+    def attend_part(query, keys, places):
         def head(part, values):
             scores = lax.dot_general(
                 part, keys, (((1,), (1,)), ((), ())), preferred_element_type=jnp.float32
             )
             top = jnp.max(scores, axis=-1, keepdims=True)
             weight = jnp.exp(scores - top).astype(jnp.bfloat16)
-            return matmul(weight, values[...])
-
-        left = head(jnp.where(low, query, zero), value_low)
-        right = head(jnp.where(low, zero, query), value_high)
+            return matmul(weight, values[places, :]), top
+
+        left, left_top = head(jnp.where(low, query, zero), value_low)
+        right, right_top = head(jnp.where(low, zero, query), value_high)
         mixed = jnp.where(low, left, right)
         total = jnp.where(
             low, pltpu.roll(left, HEAD_DIM, 1), pltpu.roll(right, HEAD_DIM, 1)
         )
+        return mixed, total, jnp.where(low, left_top, right_top)
+
+    def attend(query, keys):
+        mixed, total, _ = attend_part(query, keys, pl.ds(0, n * rows))
         return (mixed / total).astype(jnp.bfloat16)
 
     wait_all(
@@ -460,42 +465,68 @@
     loads[6].wait()
     wait_all(HEAD, lambda s: head_send.at[s], lambda s: head_recv.at[:, column(s)])
 
-    @pl.loop(0, blocks)
-    def _(i):
-        mixed = matmul(head_recv[...], weights[3, :, wide(i)])
-        encoded[:, wide(i)] = (doc[:, wide(i)].astype(jnp.float32) + mixed).astype(jnp.bfloat16)
-
     own_refs = Reduction(near, OWN_PARTS, own_full, *grad_refs[:REFS])
     cross_refs = Reduction(near, CROSS_PARTS, cross_full, *grad_refs[REFS:])
-
-    normed[...] = norm_rows(encoded[...], memory_gain[...])
     loads[7].wait()
     loads[8].wait()
 
-    @pl.loop(0, blocks)
-    def _(i):
-        block = lax.rem(lax.div(me, 2) + (blocks - 1) - i, blocks)
-        for t in range(2):
-            part = matmul(normed[...], weights[5 + t, :, wide(block)]).astype(jnp.bfloat16)
-            kv_send[2 * block, t] = part[:, :LANES]
-            kv_send[2 * block + 1, t] = part[:, LANES:]
-        for half in range(2):
-            peer = 2 * block + half
-            start(KV, peer, kv_send.at[peer], kv_recv.at[:, me])
+    for side, phase in enumerate((KV, KV_LATE)):
+        place = pl.ds(side * (rows // 2), rows // 2)
+
+        @pl.loop(0, blocks)
+        def _(i):
+            mixed = matmul(head_recv[place, :], weights[3, :, wide(i)])
+            total = doc[place, wide(i)].astype(jnp.float32) + mixed
+            encoded[place, wide(i)] = total.astype(jnp.bfloat16)
+
+        normed[place, :] = norm_rows(encoded[place, :], memory_gain[...])
+
+        @pl.loop(0, blocks)
+        def _(i):
+            block = lax.rem(lax.div(me, 2) + (blocks - 1) - i, blocks)
+            for t in range(2):
+                part = matmul(normed[place, :], weights[5 + t, :, wide(block)]).astype(jnp.bfloat16)
+                kv_send[2 * block, side, t] = part[:, :LANES]
+                kv_send[2 * block + 1, side, t] = part[:, LANES:]
+            for half in range(2):
+                peer = 2 * block + half
+                start(phase, peer, kv_send.at[peer, side], kv_recv.at[side, :, me])
 
     loads[9].wait()
     own_refs.product(head_recv, own_cotangent)
     own_refs.pair_sum()
 
     wait_all(SQ, lambda s: sq_send.at[s], lambda s: sq_recv.at[s])
-    wait_all(KV, lambda s: kv_send.at[s], lambda s: kv_recv.at[:, s])
-    set_values(kv_recv.at[1])
+    span = n * rows // 2
+
+    def ready(side, phase):
+        wait_all(phase, lambda s: kv_send.at[s, side], lambda s: kv_recv.at[side, :, s])
+        values = kv_recv[side, 1].reshape(span, LANES)
+        value_low[pl.ds(side * span, span), :] = jnp.where(low, values, one)
+        value_high[pl.ds(side * span, span), :] = jnp.where(low, one, values)
+
+    def cross_part(pair, side):
+        query = sq_recv[pl.ds(2 * pair, 2)].reshape(2 * count, LANES)
+        keys = kv_recv[side, 0].reshape(span, LANES)
+        return attend_part(query, keys, pl.ds(side * span, span))
+
+    ready(0, KV)
+
+    @pl.loop(0, n // 2)
+    def _(pair):
+        for t, value in enumerate(cross_part(pair, 0)):
+            early[t, pair] = value
+
+    ready(1, KV_LATE)
 
     def cross_block(i):
         pair = lax.rem(lax.div(me, 2) + 1 + i, n // 2)
-        keys = kv_recv[0].reshape(n * rows, LANES)
-        query = sq_recv[pl.ds(2 * pair, 2)].reshape(2 * count, LANES)
-        mixed = attend(query, keys)
+        mixed, total, top = cross_part(pair, 1)
+        best = jnp.maximum(top, early[2, pair])
+        fade, late = jnp.exp(early[2, pair] - best), jnp.exp(top - best)
+        mixed = mixed * late + early[0, pair] * fade
+        total = total * late + early[1, pair] * fade
+        mixed = (mixed / total).astype(jnp.bfloat16)
         cross_send[2 * pair] = mixed[:count]
         cross_send[2 * pair + 1] = mixed[count:]
         for half in range(2):
@@ -528,8 +559,20 @@
     wait_sent(SELF_Q, lambda p: qkv_send.at[p, 0], lambda p: qkv_recv.at[0, me])
     wait_sent(SQ, lambda p: sq_send.at[p], lambda p: sq_recv.at[me])
     wait_sent(HEAD, lambda p: head_send.at[p], lambda p: head_recv.at[:, column(me)])
-    wait_sent(KV, lambda p: kv_send.at[p], lambda p: kv_recv.at[:, me])
+    for side, phase in enumerate((KV, KV_LATE)):
+        wait_sent(phase, lambda p: kv_send.at[p, side], lambda p: kv_recv.at[side, :, me])
     wait_sent(CROSS, lambda p: cross_send.at[p], lambda p: cross_recv.at[:, column(me)])
+
+
+def store_kernel(*refs):
+    copies = [
+        pltpu.make_async_copy(src, dst, refs[8].at[i])
+        for i, (src, dst) in enumerate(zip(refs[:4], refs[4:8]))
+    ]
+    for copy in copies:
+        copy.start()
+    for copy in copies:
+        copy.wait()
 
 
 def solution(mesh):
@@ -558,7 +601,7 @@
         hbm = pl.BlockSpec(memory_space=pl.ANY)
         vmem = pl.BlockSpec(memory_space=pltpu.VMEM)
         shapes = [(rows, width), (count, width), (width, width), (width, width)]
-        encoded, decoded, own_grad, cross_grad = pl.pallas_call(
+        results = pl.pallas_call(
             functools.partial(layer_kernel, n),
             out_shape=[pltpu.VMEM(shape, half) for shape in shapes],
             in_specs=[hbm] * 2 + [vmem] * 3 + [hbm] * 10,
@@ -576,15 +619,16 @@
                 pltpu.VMEM((n, count, LANES), half),
                 pltpu.VMEM((n, rows, LANES), half),
                 pltpu.VMEM((rows, width), half),
-                pltpu.VMEM((n, 2, rows, LANES), half),
-                pltpu.VMEM((2, n, rows, LANES), half),
+                pltpu.VMEM((n, 2, 2, rows // 2, LANES), half),
+                pltpu.VMEM((2, 2, n, rows // 2, LANES), half),
+                pltpu.VMEM((3, n // 2, 2 * count, LANES), jnp.float32),
                 pltpu.VMEM((n, count, LANES), half),
                 pltpu.VMEM((count, width), half),
                 pltpu.VMEM((n * rows, LANES), half),
                 pltpu.VMEM((n * rows, LANES), half),
                 pltpu.SemaphoreType.DMA((12,)),
-                pltpu.SemaphoreType.DMA((6, n)),
-                pltpu.SemaphoreType.DMA((6, n)),
+                pltpu.SemaphoreType.DMA((7, n)),
+                pltpu.SemaphoreType.DMA((7, n)),
                 *reduction_scratch(OWN_PARTS, width),
                 *reduction_scratch(CROSS_PARTS, width),
             ],
@@ -608,6 +652,14 @@
             encoder_cotangent[0],
             decoder_cotangent[0],
         )
+        encoded, decoded, own_grad, cross_grad = pl.pallas_call(
+            store_kernel,
+            out_shape=[jax.ShapeDtypeStruct(shape, half) for shape in shapes],
+            in_specs=[vmem] * 4,
+            out_specs=[hbm] * 4,
+            scratch_shapes=[pltpu.SemaphoreType.DMA((4,))],
+            compiler_params=pltpu.CompilerParams(vmem_limit_bytes=4 * 2**20),
+        )(*[pltpu.with_memory_space_constraint(result, pltpu.VMEM) for result in results])
         return (
             encoded[None],
             decoded[None],

time: 114 us -> 106 us (0.930)
  local copies, waits for them, and re-layouts: 4.13 us -> 0 us
  Pallas kernels: 109 us -> 105 us
    pallas_call x1, Pallas kernels: 109 us -> 103 us  [body(): pl.pallas_call(functools.partial(layer_kernel, n), out_shape=[pltpu.VMEM(...]
    unnamed x4 -> x0, local copies, waits for them, and re-layouts: 4.13 us -> none
    pallas_call x0 -> x1, Pallas kernels: none -> 2.31 us  [body(): pl.pallas_call(store_kernel, out_shape=[jax.ShapeDtypeStruct(shape, half)...]
where the time goes in v5:
time: 106 us
  Pallas kernels  105 us (99%)
    pallas_call x1, Pallas kernels, body(): pl.pallas_call(functools.partial(layer_kernel, n), out_shape=[pltpu.VMEM(...  103 us
    pallas_call x1, Pallas kernels, body(): pl.pallas_call(store_kernel, out_shape=[jax.ShapeDtypeStruct(shape, half)...  2.31 us

profile of v5, /device:TPU:1, one launch (start us, length us, event | category | flops | bytes accessed | tf_op | source)
XLA Modules:
  0.0 106.1 jit_solution(6302560057615841215)
XLA Ops:
  0.6 103.0 %shard_map.174 = (bf16[256,1024]{1,0:T(8,128)(2,1)S(1)}, bf16[128,1024]{1,0:T(8,128)(2,1)S(1)}, bf16[1024,1024]{1,0:T(8,128)(2,1)S(1)}, bf16[1024,1024]{1,0:T(8,128)(2,1)S(1)}) custom-call(bf16[256,1024]{1,0:T(8,128)(2,1)} %bitcast.9, bf16[128,1024]{1,0:T(8,128)(2,1)} %bitcast.11, f32[1,1024]{1,0:T(1,128)} %bitcast.13, f32[1,1024]{1,0:T(1,128)} %bitcast.14, ...), custom_call_target="tpu_custom_call" | custom-call | tf_op jit(solution)/shard_map/pallas_call | solution.py:604
  103.6 2.3 %shard_map.175 = (bf16[256,1024]{1,0:T(8,128)(2,1)}, bf16[128,1024]{1,0:T(8,128)(2,1)}, bf16[1024,1024]{1,0:T(8,128)(2,1)}, bf16[1024,1024]{1,0:T(8,128)(2,1)}) custom-call(bf16[256,1024]{1,0:T(8,128)(2,1)S(1)} %get-tuple-element.12.refs_0_, bf16[128,1024]{1,0:T(8,128)(2,1)S(1)} %get-tuple-element.13.refs_1_, ...), custom_call_target="tpu_custom_call" | custom-call | tf_op jit(solution)/shard_map/pallas_call | solution.py:655

commit v6 on v5

--- a/solution.py
+++ b/solution.py
@@ -195,25 +195,25 @@
                 self.arrived(("last", part, k), place)
                 self.copy(("across", part, k), place, place, self.near.sibling).start()
 
+    def early_left(self):
+        for i in range(self.half // 256):
+            self.left(("pair", i), self.pair.at[pl.ds(i * 256, 256)])
+        for part, (start, width, axis) in enumerate(self.parts):
+            self.left(("first", part), self.first_in.at[:, :, pl.ds(start, width)])
+            self.left(("second", part), self.second_in.at[:, :, self.landing(part)])
+
     def finish(self):
         turn = self.other - self.base
         for part, (start, width, axis) in enumerate(self.parts):
             cols = pl.ds(start, width)
-            for k in range(4):
-                rows = aligned(self.own_rows(part, k) + turn, self.size)
-                self.arrived(("across", part, k), self.full.at[rows, cols])
-        for part, (start, width, axis) in enumerate(self.parts):
-            cols = pl.ds(start, width)
-            self.left(("first", part), self.first_in.at[:, :, cols])
-            self.left(("second", part), self.second_in.at[:, :, self.landing(part)])
             self.left(("back", part), self.second_in.at[:, :, self.landing(part)])
             block = self.full.at[pl.ds(0, self.size), cols]
             for k in (1, 2, 3):
                 self.left(("last", part, k), block)
             for k in range(4):
+                rows = aligned(self.own_rows(part, k) + turn, self.size)
+                self.arrived(("across", part, k), self.full.at[rows, cols])
                 self.left(("across", part, k), block)
-        for i in range(self.half // 256):
-            self.left(("pair", i), self.pair.at[pl.ds(i * 256, 256)])
 
 
 def reduction_scratch(parts, width):
@@ -552,16 +552,18 @@
     cross_refs.scatter_first()
     cross_refs.scatter_second()
     own_refs.gather_first()
-    cross_refs.gather_second()
-    cross_refs.gather_first()
-    own_refs.finish()
-    cross_refs.finish()
     wait_sent(SELF_Q, lambda p: qkv_send.at[p, 0], lambda p: qkv_recv.at[0, me])
     wait_sent(SQ, lambda p: sq_send.at[p], lambda p: sq_recv.at[me])
     wait_sent(HEAD, lambda p: head_send.at[p], lambda p: head_recv.at[:, column(me)])
     for side, phase in enumerate((KV, KV_LATE)):
         wait_sent(phase, lambda p: kv_send.at[p, side], lambda p: kv_recv.at[side, :, me])
     wait_sent(CROSS, lambda p: cross_send.at[p], lambda p: cross_recv.at[:, column(me)])
+    cross_refs.gather_second()
+    own_refs.early_left()
+    cross_refs.early_left()
+    own_refs.finish()
+    cross_refs.gather_first()
+    cross_refs.finish()
 
 
 def store_kernel(*refs):

time: 106 us -> 106 us (level)
  no operation moved by 1% of the time
where the time goes in v6:
time: 106 us
  Pallas kernels  105 us (99%)
    pallas_call x1, Pallas kernels, body(): pl.pallas_call(functools.partial(layer_kernel, n), out_shape=[pltpu.VMEM(...  102 us
    pallas_call x1, Pallas kernels, body(): pl.pallas_call(store_kernel, out_shape=[jax.ShapeDtypeStruct(shape, half)...  2.31 us

profile of v6, /device:TPU:1, one launch (start us, length us, event | category | flops | bytes accessed | tf_op | source)
XLA Modules:
  0.0 105.6 jit_solution(11084048634160872764)
XLA Ops:
  0.6 102.5 %shard_map.174 = (bf16[256,1024]{1,0:T(8,128)(2,1)S(1)}, bf16[128,1024]{1,0:T(8,128)(2,1)S(1)}, bf16[1024,1024]{1,0:T(8,128)(2,1)S(1)}, bf16[1024,1024]{1,0:T(8,128)(2,1)S(1)}) custom-call(bf16[256,1024]{1,0:T(8,128)(2,1)} %bitcast.9, bf16[128,1024]{1,0:T(8,128)(2,1)} %bitcast.11, f32[1,1024]{1,0:T(1,128)} %bitcast.13, f32[1,1024]{1,0:T(1,128)} %bitcast.14, ...), custom_call_target="tpu_custom_call" | custom-call | tf_op jit(solution)/shard_map/pallas_call | solution.py:606
  103.1 2.3 %shard_map.175 = (bf16[256,1024]{1,0:T(8,128)(2,1)}, bf16[128,1024]{1,0:T(8,128)(2,1)}, bf16[1024,1024]{1,0:T(8,128)(2,1)}, bf16[1024,1024]{1,0:T(8,128)(2,1)}) custom-call(bf16[256,1024]{1,0:T(8,128)(2,1)S(1)} %get-tuple-element.12.refs_0_, bf16[128,1024]{1,0:T(8,128)(2,1)S(1)} %get-tuple-element.13.refs_1_, ...), custom_call_target="tpu_custom_call" | custom-call | tf_op jit(solution)/shard_map/pallas_call | solution.py:657

commit v7 on v6

--- a/solution.py
+++ b/solution.py
@@ -551,7 +551,6 @@
     own_refs.gather_second()
     cross_refs.scatter_first()
     cross_refs.scatter_second()
-    own_refs.gather_first()
     wait_sent(SELF_Q, lambda p: qkv_send.at[p, 0], lambda p: qkv_recv.at[0, me])
     wait_sent(SQ, lambda p: sq_send.at[p], lambda p: sq_recv.at[me])
     wait_sent(HEAD, lambda p: head_send.at[p], lambda p: head_recv.at[:, column(me)])
@@ -559,6 +558,7 @@
         wait_sent(phase, lambda p: kv_send.at[p, side], lambda p: kv_recv.at[side, :, me])
     wait_sent(CROSS, lambda p: cross_send.at[p], lambda p: cross_recv.at[:, column(me)])
     cross_refs.gather_second()
+    own_refs.gather_first()
     own_refs.early_left()
     cross_refs.early_left()
     own_refs.finish()

time: 106 us -> 106 us (level)
  no operation moved by 1% of the time
where the time goes in v7:
time: 106 us
  Pallas kernels  105 us (99%)
    pallas_call x1, Pallas kernels, body(): pl.pallas_call(functools.partial(layer_kernel, n), out_shape=[pltpu.VMEM(...  102 us
    pallas_call x1, Pallas kernels, body(): pl.pallas_call(store_kernel, out_shape=[jax.ShapeDtypeStruct(shape, half)...  2.31 us

profile of v7, /device:TPU:1, one launch (start us, length us, event | category | flops | bytes accessed | tf_op | source)
XLA Modules:
  0.0 105.6 jit_solution(912135319940461178)
XLA Ops:
  0.6 102.5 %shard_map.174 = (bf16[256,1024]{1,0:T(8,128)(2,1)S(1)}, bf16[128,1024]{1,0:T(8,128)(2,1)S(1)}, bf16[1024,1024]{1,0:T(8,128)(2,1)S(1)}, bf16[1024,1024]{1,0:T(8,128)(2,1)S(1)}) custom-call(bf16[256,1024]{1,0:T(8,128)(2,1)} %bitcast.9, bf16[128,1024]{1,0:T(8,128)(2,1)} %bitcast.11, f32[1,1024]{1,0:T(1,128)} %bitcast.13, f32[1,1024]{1,0:T(1,128)} %bitcast.14, ...), custom_call_target="tpu_custom_call" | custom-call | tf_op jit(solution)/shard_map/pallas_call | solution.py:606
  103.1 2.3 %shard_map.175 = (bf16[256,1024]{1,0:T(8,128)(2,1)}, bf16[128,1024]{1,0:T(8,128)(2,1)}, bf16[1024,1024]{1,0:T(8,128)(2,1)}, bf16[1024,1024]{1,0:T(8,128)(2,1)}) custom-call(bf16[256,1024]{1,0:T(8,128)(2,1)S(1)} %get-tuple-element.12.refs_0_, bf16[128,1024]{1,0:T(8,128)(2,1)S(1)} %get-tuple-element.13.refs_1_, ...), custom_call_target="tpu_custom_call" | custom-call | tf_op jit(solution)/shard_map/pallas_call | solution.py:657
